TPU v7x, 32 devices: a whole 2x2x4 slice. The times are simulated.
32 devices in a mesh: clip: 2 (over x), tm: 4 (over z), chan: 4 (over y, core).
Axes of the slice: x: 2, y: 2, z: 4, core: 2. Of those that a mesh axis runs over, the one named last changes fastest.
Arguments:
- signal: bfloat16 [2, 4096, 256], P('clip', 'tm', 'chan'), may hold values from -6 to 6
- conv_first: bfloat16 [3, 256, 128], P(None, 'chan'), may hold values from -0.21875 to 0.21875
- conv_second: bfloat16 [128, 256], P(None, 'chan'), may hold values from -0.5 to 0.5
- conv_down: bfloat16 [16, 256, 512], P(None, 'chan'), may hold values from -0.09375 to 0.09375
- cotangent: bfloat16 [2, 512, 512], P('clip', 'tm'), may hold values from -6 to 6
Outputs:
- grad_signal: bfloat16 [2, 4096, 256], P('clip', 'tm', 'chan')
- grad_first: float32 [3, 256, 128], P(None, 'chan')
- grad_second: float32 [128, 256], P(None, 'chan')
- grad_down: float32 [16, 256, 512], P(None, 'chan')
All inputs are finite; a program needn't handle non-finite values.
Results may differ from a plain program's by a relative error of at most 0.018.
Values may be sent and summed in bfloat16 or wider, within the bound.
No kernel may reach another device: no remote copies, remote signals or barrier semaphores. Data moves between devices by JAX's collectives and lax.ppermute only.
A program may use at most 64 MiB of HBM per device.

v0:
```python
import jax
import jax.numpy as jnp
from jax import lax
from jax.sharding import PartitionSpec as P

KRES = 3
STRIDE = 8
RIM = 10


def shifted(block, axis, distance):
    devices = range(lax.axis_size(axis))
    route = [(i - distance, i) for i in devices if i - distance in devices]
    return lax.ppermute(block, axis, route)


def elu(value):
    return jnp.where(value > 0, value, jnp.exp(jnp.minimum(value, 0.0)) - 1.0)


def slope(value):
    return jnp.where(value > 0, 1.0, jnp.exp(jnp.minimum(value, 0.0)))


def contract_rows(left, right):
    return lax.dot_general(
        left, right, (((0,), (0,)), ((), ())), preferred_element_type=jnp.float32
    )


def contract_cols(left, right):
    return lax.dot_general(
        left, right, (((1,), (1,)), ((), ())), preferred_element_type=jnp.float32
    )


def causal_conv(values, weights, span):
    total = jnp.zeros((span, weights.shape[2]), jnp.float32)
    for k in range(KRES):
        total = total + jnp.dot(
            values[k : k + span], weights[k], preferred_element_type=jnp.float32
        )
    return total


def on_device(signal, conv_first, conv_second, conv_down, cotangent):
    frames = signal[0]
    length, local_ch = frames.shape
    span = length + RIM - KRES + 1
    borrowed = shifted(frames[length - RIM :], "tm", 1)
    padded = jnp.concatenate([borrowed, frames], axis=0)
    act = elu(padded.astype(jnp.float32)).astype(jnp.bfloat16)
    hidden = lax.psum(causal_conv(act, conv_first, span).astype(jnp.bfloat16), "chan").astype(
        jnp.float32
    )
    inner = elu(hidden).astype(jnp.bfloat16)
    resid = padded[KRES - 1 :].astype(jnp.float32) + jnp.dot(
        inner, conv_second, preferred_element_type=jnp.float32
    )
    feed = elu(resid).astype(jnp.bfloat16)
    blocks = feed.reshape(span // STRIDE, STRIDE * local_ch)
    wide = conv_down.reshape(2, STRIDE * local_ch, conv_down.shape[2])
    upstream = cotangent[0]
    count = upstream.shape[0]
    front = contract_cols(upstream, wide[0])
    back = contract_cols(upstream, wide[1])
    dblocks = jnp.pad(front, ((0, 1), (0, 0))) + jnp.pad(back, ((1, 0), (0, 0)))
    down_raw = jnp.stack(
        [contract_rows(blocks[:count], upstream), contract_rows(blocks[1:], upstream)]
    )
    down_raw = down_raw.reshape(conv_down.shape)
    dresid = dblocks.reshape(span, local_ch) * slope(resid)
    dres16 = dresid.astype(jnp.bfloat16)
    second_raw = contract_rows(inner, dres16)
    dinner = lax.psum(contract_cols(dres16, conv_second).astype(jnp.bfloat16), "chan").astype(
        jnp.float32
    )
    dhid = (dinner * slope(hidden)).astype(jnp.bfloat16)
    first_raw = jnp.stack([contract_rows(act[k : k + span], dhid) for k in range(KRES)])
    dact = jnp.zeros(padded.shape, jnp.float32)
    for k in range(KRES):
        dact = dact + jnp.pad(contract_cols(dhid, conv_first[k]), ((k, KRES - 1 - k), (0, 0)))
    dpadded = dact * slope(padded.astype(jnp.float32)) + jnp.pad(dresid, ((KRES - 1, 0), (0, 0)))
    returned = shifted(dpadded[:RIM], "tm", -1)
    grad_frames = dpadded[RIM:] + jnp.pad(returned, ((length - RIM, 0), (0, 0)))
    first_total, second_total, down_total = lax.psum(
        (first_raw, second_raw, down_raw), ("clip", "tm")
    )
    factor = 1.0 / jnp.sqrt(
        jnp.float32(lax.axis_size("clip") * lax.axis_size("tm") * (length // STRIDE))
    )
    return (
        grad_frames.astype(jnp.bfloat16)[None],
        first_total * factor,
        second_total * factor,
        down_total * factor,
    )


def solution(mesh):
    return jax.shard_map(
        on_device,
        mesh=mesh,
        in_specs=(
            P("clip", "tm", "chan"),
            P(None, "chan", None),
            P(None, "chan"),
            P(None, "chan", None),
            P("clip", "tm", None),
        ),
        out_specs=(
            P("clip", "tm", "chan"),
            P(None, "chan", None),
            P(None, "chan"),
            P(None, "chan", None),
        ),
        check_vma=False,
    )
```

profile of v0, /device:TPU:0, one launch (start us, length us, event | category | flops | bytes accessed | tf_op | source)
XLA Modules:
  0.0 208.7 jit_solution(13187131113075802272)
XLA Ops:
  7.2 0.9 slice_bitcast_fusion
  8.1 4.9 %collective-permute-start = (bf16[10,64]{0,1:T(8,128)(2,1)S(1)}, bf16[10,64]{0,1:T(8,128)(2,1)S(1)}, u32[]{:S(2)}, u32[]{:S(2)}) collective-permute-start(bf16[10,64]{0,1:T(8,128)(2,1)S(1)} %slice_bitcast_fusion), channel_id=1, source_target_pairs={{0,4},{4,8},{8,12},{1,5},{5,9},{9,13},{2,6},{6,10},{10,14},{3,7},{... | collective-permute-start | bytes 3848 | tf_op jit(solution)/shard_map/ppermute | solution.py:14
  13.0 1.3 fusion.56
  14.3 0.3 fusion.22
  14.8 0.3 fusion.29
  15.2 0.5 convolution_add_fusion.1
  15.6 1.2 fusion
  16.9 0.3 fusion.20
  17.6 32.4 %all-reduce.12.cloned.1.call-done = bf16[1032,128]{1,0:T(8,128)(2,1)} async-done(((bf16[1032,128]{1,0:T(8,128)(2,1)}), bf16[1032,128]{1,0:T(8,128)(2,1)}) %all-reduce.12.cloned.1.call-update) | async-done | bytes 264208 | tf_op jit(solution)/shard_map/psum | solution.py:53
  50.0 1.3 fusion.9
  52.2 1.0 convolution_convert_fusion
  53.3 0.3 convolution_bitcast_fusion
  53.6 0.3 convolution_bitcast_fusion.1
  54.0 1.5 pad_maximum_fusion
  55.4 30.2 %all-reduce.14.cloned.1.call-done = bf16[1032,128]{1,0:T(8,128)(2,1)} async-done(((bf16[1032,128]{1,0:T(8,128)(2,1)}), bf16[1032,128]{1,0:T(8,128)(2,1)}) %all-reduce.14.cloned.1.call-update) | async-done | bytes 264208 | tf_op jit(solution)/shard_map/psum | solution.py:75
  85.6 1.1 fusion.3
  86.7 0.2 convolution_bitcast_fusion.2
  87.0 0.2 convolution_bitcast_fusion.3
  87.4 0.7 pad_maximum_fusion.2
  88.1 0.3 fusion.31
  88.4 39.2 %psum.38 = f32[128,64]{0,1:T(8,128)S(1)} all-reduce(f32[128,64]{0,1:T(8,128)S(1)} %fusion.31), channel_id=1, replica_groups=mesh['clip'=2,'tm'=4,'chan'=4] {'clip','tm'}, use_global_device_ids=true, to_apply=%region_3.4 | all-reduce | flops 8192 | bytes 65536 | tf_op jit(solution)/shard_map/psum | solution.py:86
  127.6 0.2 fusion.37
  127.8 0.2 fusion.40
  128.0 0.2 fusion.43
  128.2 0.3 fusion.11
  128.6 1.3 collective-permute-start.1
  129.9 0.6 broadcast_multiply_fusion.2
  130.5 3.9 %collective-permute-done.1 = f32[10,64]{0,1:T(8,128)S(1)} collective-permute-done((f32[10,64]{0,1:T(8,128)S(1)}, f32[10,64]{0,1:T(8,128)S(1)}, u32[]{:S(2)}, u32[]{:S(2)}) %collective-permute-start.1) | collective-permute-done | bytes 2592 | tf_op jit(solution)/shard_map/ppermute | solution.py:14
  134.4 0.8 fusion.17
  135.2 62.3 %all-reduce.16.cloned.1.call-done = (f32[3,64,128]{2,1,0:T(8,128)}, f32[16,64,512]{2,1,0:T(8,128)}) async-done(((f32[3,64,128]{2,1,0:T(8,128)}, f32[16,64,512]{2,1,0:T(8,128)}), (f32[3,64,128]{2,1,0:T(8,128)}, f32[16,64,512]{2,1,0:T(8,128)})) %all-reduce.16.cloned.1.call-update) | async-done | bytes 2195472 | tf_op jit(solution)/shard_map/psum | solution.py:86
  197.5 1.5 broadcast_multiply_fusion.1
  199.0 3.2 %broadcast_multiply_fusion = f32[16,64,512]{2,1,0:T(8,128)} fusion(f32[16,64,512]{2,1,0:T(8,128)} %get-tuple-element.5), kind=kLoop, calls=%fused_computation.10 | loop fusion | flops 524288 | bytes 4194304 | tf_op jit(solution)/shard_map/mul | solution.py:96
  (28 shorter events, 1.8 us)
Async XLA Ops:
  7.2 7.2 %copy-start = (bf16[1,128,512]{2,1,0:T(8,128)(2,1)S(1)}, bf16[1,128,512]{2,1,0:T(8,128)(2,1)}, u32[]{:S(2)}) copy-start(bf16[1,128,512]{2,1,0:T(8,128)(2,1)} %param.9) | copy-start | bytes 393220
  7.2 7.5 %copy-start.1 = (bf16[1,1024,64]{1,2,0:T(8,128)(2,1)S(1)}, bf16[1,1024,64]{1,2,0:T(8,128)(2,1)}, u32[]{:S(2)}) copy-start(bf16[1,1024,64]{1,2,0:T(8,128)(2,1)} %param.5) | copy-start | bytes 393220
  7.2 7.6 %copy-start.3 = (bf16[3,64,128]{2,1,0:T(8,128)(2,1)S(1)}, bf16[3,64,128]{2,1,0:T(8,128)(2,1)}, u32[]{:S(2)}) copy-start(bf16[3,64,128]{2,1,0:T(8,128)(2,1)} %param.6) | copy-start | bytes 147460
  7.2 42.8 %all-reduce.12.cloned.1.call-start = ((), (), s32[]{:S(2)}) async-start(), calls=%async_computation | async-start | bytes 528384 | tf_op jit(solution)/shard_map/psum | solution.py:53
  8.1 6.5 %collective-permute-start = (bf16[10,64]{0,1:T(8,128)(2,1)S(1)}, bf16[10,64]{0,1:T(8,128)(2,1)S(1)}, u32[]{:S(2)}, u32[]{:S(2)}) collective-permute-start(bf16[10,64]{0,1:T(8,128)(2,1)S(1)} %slice_bitcast_fusion), channel_id=1, source_target_pairs={{0,4},{4,8},{8,12},{1,5},{5,9},{9,13},{2,6},{6,10},{10,14},{3,7},{... | collective-permute-start | bytes 3848 | tf_op jit(solution)/shard_map/ppermute | solution.py:14
  15.6 34.4 %copy-start.4 = (bf16[128,64]{0,1:T(8,128)(2,1)S(1)}, bf16[128,64]{0,1:T(8,128)(2,1)}, u32[]{:S(2)}) copy-start(bf16[128,64]{0,1:T(8,128)(2,1)} %param.7) | copy-start | bytes 49156
  16.8 68.8 %all-reduce.14.cloned.1.call-start = ((), (), s32[]{:S(2)}) async-start(), calls=%async_computation.1 | async-start | bytes 528384 | tf_op jit(solution)/shard_map/psum | solution.py:75
  53.3 144.2 %all-reduce.16.cloned.1.call-start = ((), (), s32[]{:S(2)}) async-start(), calls=%async_computation.2 | async-start | bytes 4390912 | tf_op jit(solution)/shard_map/psum | solution.py:86
  53.9 31.7 %copy-start.2 = (bf16[1032,128]{1,0:T(8,128)(2,1)S(1)}, bf16[1032,128]{1,0:T(8,128)(2,1)}, u32[]{:S(2)}) copy-start(bf16[1032,128]{1,0:T(8,128)(2,1)} %all-reduce.12.cloned.1.call-done) | copy-start | bytes 792580
  128.6 5.8 %collective-permute-start.1 = (f32[10,64]{0,1:T(8,128)S(1)}, f32[10,64]{0,1:T(8,128)S(1)}, u32[]{:S(2)}, u32[]{:S(2)}) collective-permute-start(f32[10,64]{0,1:T(8,128)S(1)} %slice.82), channel_id=1, source_target_pairs={{4,0},{8,4},{12,8},{5,1},{9,5},{13,9},{6,2},{10,6},{14,10},{7,3},{... | collective-permute-start | bytes 7688 | tf_op jit(solution)/shard_map/ppermute | solution.py:14
Sparse Core Ops, SparseCore 0:
  16.9 32.9 all-reduce.11
  53.4 32.2 all-reduce.13
  90.0 107.4 all-reduce.15
where the time goes:
time: 209 us
  waiting for transfers between devices  129 us (62%)
  blocking collectives  39.2 us (19%)
  between operations  13.9 us (7%)
  other arithmetic  9.89 us (5%)
  matrix products  7.15 us (3%)
  starting transfers between devices  6.33 us (3%)
  local copies, waits for them, and re-layouts  3.4 us (2%)
    psum x1, waiting for transfers between devices, on_device(): lax.psum((first_raw, second_raw, down_raw), ('clip', 'tm'))  62.3 us
    psum x1, blocking collectives, on_device(): lax.psum((first_raw, second_raw, down_raw), ('clip', 'tm'))  39.2 us
    psum x1, waiting for transfers between devices, on_device(): lax.psum(causal_conv(act, conv_first, span).astype(jnp.bfloat16), 'chan')  32.4 us
    psum x1, waiting for transfers between devices, on_device(): lax.psum(contract_cols(dres16, conv_second).astype(jnp.bfloat16), 'chan')  30.2 us
    ppermute x2, starting transfers between devices, shifted(): return lax.ppermute(block, axis, route)  6.21 us
  transfers between devices with their start and end apart: 5, of which 4 were waited for; matrix products, arithmetic and copies ran while one was open for 3% of the time, Pallas kernels for 0%

commit v1 on v0

v1 whole, which is shorter than its diff:
```python
import jax
import jax.numpy as jnp
import numpy as np
from jax import lax
from jax.experimental import pallas as pl
from jax.experimental.pallas import tpu as pltpu
from jax.sharding import PartitionSpec as P

KRES = 3
STRIDE = 8
LANE = 128
F32 = jnp.float32
BF16 = jnp.bfloat16


def dot(left, right, dims=((1,), (0,))):
    return lax.dot_general(left, right, (dims, ((), ())), preferred_element_type=F32)


def elu(value):
    return jnp.where(value > 0, value, jnp.exp(jnp.minimum(value, 0.0)) - 1.0)


def slope(value):
    return jnp.where(value > 0, 1.0, jnp.exp(jnp.minimum(value, 0.0)))


def lane_of(shape):
    return lax.broadcasted_iota(jnp.int32, shape, 1)


def roll(value, shift):
    return pltpu.roll(value, shift % value.shape[1], 1)


def swap_chunks(blocks):
    chunk = lane_of(blocks[0].shape) // 16
    blocks = list(blocks)
    for s in (1, 2, 4):
        low = (chunk & s) == 0
        new = list(blocks)
        for i in range(8):
            if i & s == 0:
                a, b = blocks[i], blocks[i | s]
                new[i] = jnp.where(low, a, roll(b, 16 * s))
                new[i | s] = jnp.where(low, roll(a, -16 * s), b)
        blocks = new
    return blocks


def interleaver():
    row = lax.broadcasted_iota(jnp.int32, (LANE, LANE), 0)
    col = lax.broadcasted_iota(jnp.int32, (LANE, LANE), 1)
    return jnp.where(col == 16 * (row % 8) + row // 8, 1.0, 0.0).astype(BF16)


def to_phase(blocks):
    rows = blocks[0].shape[0]
    mixed = dot(jnp.concatenate(blocks, axis=0), interleaver())
    return swap_chunks([mixed[rows * b : rows * (b + 1)] for b in range(8)])


def to_time(blocks):
    rows = blocks[0].shape[0]
    mixed = jnp.concatenate(swap_chunks(blocks), axis=0).astype(BF16)
    out = dot(mixed, interleaver(), ((1,), (1,)))
    return [out[rows * b : rows * (b + 1)] for b in range(8)]


def cut(value, n=8):
    return [value[:, LANE * k : LANE * (k + 1)] for k in range(n)]


def prep_kernel(sig, first, second, cot, pack, ahead, back, quarter):
    ch, length = sig.shape
    chan = lax.axis_index("chan")
    blocks = cut(sig[...])
    for k, block in enumerate(to_phase(blocks)):
        pack[:, LANE * k : LANE * (k + 1)] = block.astype(BF16)
    for k in range(KRES):
        pack[:, length + LANE * k : length + LANE * (k + 1)] = first[k]
    pack[:, length + LANE * KRES :] = second[...]
    ahead[...] = roll(blocks[7].astype(F32), 2).astype(BF16)
    back[:ch, :] = roll(blocks[0].astype(F32), 2).astype(BF16)
    head = cot[:16, :].astype(F32)
    rows = [head[r : r + 1, LANE * i : LANE * (i + 1)] for r in range(2) for i in range(4)]
    back[ch:, :] = jnp.concatenate(rows + [jnp.zeros((8, LANE), F32)], axis=0).astype(BF16)
    per = quarter.shape[0]
    quarter[...] = cot[pl.ds(pl.multiple_of(chan * per, per), per), :]


def dfeed_kernel(down, cot, ahead, back, dfeed, halo):
    ch = down.shape[1]
    width = cot.shape[1]
    tail = back[ch:, :].astype(F32)
    rows = [
        jnp.concatenate([tail[4 * r + i : 4 * r + i + 1] for i in range(4)], axis=1)
        for r in range(2)
    ]
    rows = jnp.concatenate(rows + [jnp.zeros((14, width), F32)], axis=0).astype(BF16)
    ext = jnp.concatenate(
        [cot[...], rows, jnp.zeros((LANE - 16, width), BF16)], axis=0
    )
    lane = lane_of((ch, LANE))
    ends = []
    for k in range(8):
        front = dot(down[k], ext, ((1,), (1,)))
        behind = dot(down[k + 8], ext, ((1,), (1,)))
        f0, f1 = front[:, :LANE], front[:, LANE:]
        b0, b1 = behind[:, :LANE], behind[:, LANE:]
        main = jnp.where(lane == LANE - 1, roll(f1, -1), roll(f0, -1)) + b0
        dfeed[:, LANE * k : LANE * (k + 1)] = main.astype(BF16)
        if k == 0:
            ends.append(roll(f1, -1) + b1)
        if k == 1:
            ends.append(f1 + roll(b1, 1))
    end = jnp.where(lane == 0, ends[0], jnp.where(lane == 1, ends[1], 0.0))
    dfeed[:, LANE * 8 :] = end.astype(BF16)
    near = jnp.where(lane < 2, ahead[...].astype(F32), jnp.where(lane < 4, back[:ch, :].astype(F32), 0.0))
    halo[...] = near.astype(BF16)


def forward_kernel(a0, a1, a2, a3, h0, h1, h2, h3, feed, hidden):
    packs = (a0, a1, a2, a3)
    halos = (h0, h1, h2, h3)
    ch, length = feed.shape
    taps = KRES * LANE
    act = jnp.concatenate(
        [
            jnp.concatenate([elu(a[:, :length].astype(F32)), elu(h[...].astype(F32))], axis=1)
            for a, h in zip(packs, halos)
        ],
        axis=0,
    ).astype(BF16)
    weights = jnp.concatenate([a[:, length : length + taps] for a in packs], axis=0)
    part = dot(weights, act, ((0,), (0,)))
    p0, p1, p2 = [cut(part[LANE * k : LANE * (k + 1)], 9) for k in range(KRES)]
    lane = lane_of((LANE, LANE))
    wrap6, wrap7, twice7 = roll(p0[6], 1), roll(p1[7], 1), roll(p0[7], 1)
    out = [None] * 9
    out[0] = (
        jnp.where(lane == 0, p0[8], wrap6) + jnp.where(lane == 0, roll(p1[8], -1), wrap7) + p2[0]
    )
    out[1] = jnp.where(lane == 0, roll(p0[8], -1), twice7) + p1[0] + p2[1]
    for k in range(2, 8):
        out[k] = p0[k - 2] + p1[k - 1] + p2[k]
    late = roll(p2[8], -2)
    out[8] = jnp.where(
        lane == 0,
        wrap6 + wrap7 + late,
        jnp.where(lane == 1, roll(twice7, 1) + roll(p1[8], -1) + late, 0.0),
    )
    for k in range(9):
        hidden[:, LANE * k : LANE * (k + 1)] = out[k]
    inner = elu(jnp.concatenate(out[:8], axis=1)).astype(BF16)
    resid = a0[:, :length].astype(F32) + dot(a0[:, length + taps :], inner)
    feed[...] = elu(resid).astype(BF16)


def backward_kernel(
    a0, a1, a2, a3, h0, h1, h2, h3, hidden, d0, d1, d2, d3, grad, weight
):
    packs = (a0, a1, a2, a3)
    halos = (h0, h1, h2, h3)
    grads = (d0, d1, d2, d3)
    ch, length = grad.shape
    taps = KRES * LANE
    hid = hidden[...]
    decay = jnp.exp(jnp.minimum(hid, 0.0))
    inner = jnp.where(hid > 0, hid, decay - 1.0).astype(BF16)
    hid_slope = jnp.where(hid > 0, 1.0, decay)
    mix = jnp.concatenate([a[:, length + taps :] for a in packs], axis=0)
    bent = dot(mix, inner)
    own = None
    rounded = []
    for i in range(4):
        lead = jnp.concatenate(
            [packs[i][:, :length].astype(F32), roll(halos[i][...].astype(F32), -2)], axis=1
        )
        resid = lead + bent[ch * i : ch * (i + 1)]
        dres = grads[i][...].astype(F32) * slope(resid)
        if i == 0:
            own = dres
        rounded.append(dres.astype(BF16))
    dres16 = jnp.concatenate(rounded, axis=0)
    dinner = dot(mix, dres16, ((0,), (0,)))
    dhid = (dinner * hid_slope).astype(BF16)
    weight[ch * KRES :, :] = dot(rounded[0][:, :length], inner[:, :length], ((1,), (1,))).astype(
        weight.dtype
    )
    raw = a0[:, :length].astype(F32)
    raw_decay = jnp.exp(jnp.minimum(raw, 0.0))
    act = cut(jnp.where(raw > 0, raw, raw_decay - 1.0))
    edge = elu(h0[...].astype(F32))
    lane = lane_of((ch, LANE))
    before1 = jnp.where(lane == 0, roll(edge, -1), roll(act[7], 1))
    before2 = jnp.where(lane == 0, edge, roll(act[6], 1))
    act = [v.astype(BF16) for v in [before2, before1] + act]
    stack = jnp.concatenate(
        [jnp.concatenate(act[k : k + 8], axis=1) for k in range(KRES)], axis=0
    )
    weight[: ch * KRES, :] = dot(stack, dhid[:, :length], ((1,), (1,))).astype(weight.dtype)
    taps_own = jnp.concatenate(
        [a0[:, length + LANE * k : length + LANE * (k + 1)] for k in range(KRES)], axis=0
    )
    spread = dot(taps_own, dhid)
    q0, q1, q2 = [cut(spread[ch * k : ch * (k + 1)], 9) for k in range(KRES)]
    last = lane == LANE - 1
    q1next = jnp.where(last, roll(q1[8], -1), roll(q1[0], -1))
    q0next = jnp.where(last, roll(q0[8], -1), roll(q0[0], -1))
    q0late = jnp.where(last, roll(q0[8], -2), roll(q0[1], -1))
    q0 = q0[:8] + [q0next, q0late]
    q1 = q1[:8] + [q1next]
    raw_slope = cut(jnp.where(raw > 0, 1.0, raw_decay))
    out = []
    for k in range(8):
        dact = q0[k + 2] + q1[k + 1] + q2[k]
        total = dact * raw_slope[k] + own[:, LANE * k : LANE * (k + 1)]
        out.append(total.astype(BF16).astype(F32))
    for b, block in enumerate(to_time(out)):
        grad[:, LANE * b : LANE * (b + 1)] = block.astype(BF16)


def segment(rel):
    me = lax.axis_index("clip") * lax.axis_size("tm") + lax.axis_index("tm")
    return me ^ rel


def cot_kernel(order, per_clip, q0, q1, q2, q3, out, rows):
    per = q0.shape[0] // len(order)
    width = q0.shape[1]
    chan = lax.axis_index("chan")
    for c, piece in enumerate((q0, q1, q2, q3)):
        for p, rel in enumerate(order):
            start = pl.multiple_of(segment(rel) * LANE + (chan ^ c) * per, per)
            rows[pl.ds(start, per), :] = piece[per * p : per * (p + 1), :].astype(F32)
    value = rows[...]
    out[:, :width] = value.astype(BF16)
    count = value.shape[0]
    at = lax.broadcasted_iota(jnp.int32, value.shape, 0)
    moved = jnp.where(at % per_clip == per_clip - 1, 0.0, pltpu.roll(value, count - 1, 0))
    out[:, width:] = moved.astype(BF16)


def down_kernel(order, factor, near, far, cots, out, left):
    ch = out.shape[2]
    half = len(order) // 2
    width = out.shape[3]
    for p, rel in enumerate(order):
        source = near if p < half else far
        q = p % half
        start = pl.multiple_of(segment(rel) * LANE, LANE)
        for k in range(4):
            left[ch * k : ch * (k + 1), pl.ds(start, LANE)] = source[
                ch * q : ch * (q + 1), LANE * k : LANE * (k + 1)
            ]
    total = dot(left[...], cots[...]) * factor
    for k in range(4):
        out[0, k] = total[ch * k : ch * (k + 1), width:]
        out[1, k] = total[ch * k : ch * (k + 1), :width]


def call(kernel, name, out_shape, *args, scratch=()):
    return pl.pallas_call(kernel, out_shape=out_shape, scratch_shapes=scratch, name=name)(*args)


def struct(shape, dtype=BF16):
    return jax.ShapeDtypeStruct(shape, dtype)


def down_half(index, order, factor, ch, near, far, cots, prior):
    kernel = lambda *refs: down_kernel(order, factor, *refs)
    width = cots.shape[1] // 2
    rows = cots.shape[0]
    whole = lambda v: pl.BlockSpec(v.shape, lambda i: (0,) * v.ndim)
    args = [near, far, cots]
    specs = [whole(v) for v in args]
    alias = {}
    body = kernel
    if prior is not None:
        args.append(prior)
        specs.append(pl.BlockSpec(memory_space=pl.ANY))
        alias = {3: 0}
        body = lambda n, f, c, p, o, s: kernel(n, f, c, o, s)
    return pl.pallas_call(
        body,
        grid=(1,),
        in_specs=specs,
        out_specs=pl.BlockSpec((2, 4, ch, width), lambda i: (0, index, 0, 0)),
        out_shape=struct((2, 8, ch, width), F32),
        scratch_shapes=[pltpu.VMEM((4 * ch, rows), BF16)],
        input_output_aliases=alias,
        name="down%d" % index,
    )(*args)


def along_chan(value, other):
    pairs = [(i, i ^ other) for i in range(lax.axis_size("chan"))]
    return lax.ppermute(value, "chan", pairs)


def along_group(value, other):
    count = lax.axis_size("clip") * lax.axis_size("tm")
    return lax.ppermute(value, ("clip", "tm"), [(i, i ^ other) for i in range(count)])


def shifted(value, distance):
    devices = range(lax.axis_size("tm"))
    route = [(i, i + distance) for i in devices if i + distance in devices]
    return lax.ppermute(value, "tm", route)


def after(value, *others):
    return lax.optimization_barrier((value, *others))[0]


def on_device(signal, conv_first, conv_second, conv_down, cotangent):
    sig = signal[0].T
    second = conv_second.T
    cot = cotangent[0]
    ch, length = sig.shape
    count, width = cot.shape
    clips, times = lax.axis_size("clip"), lax.axis_size("tm")
    group = clips * times
    packed = length + LANE * (KRES + 1)
    pack, ahead, back, quarter = call(
        prep_kernel,
        "prep",
        (
            struct((ch, packed)),
            struct((ch, LANE)),
            struct((ch + 16, LANE)),
            struct((count // 4, width)),
        ),
        sig,
        conv_first,
        second,
        cot,
    )
    pack_y = along_chan(pack, 2)
    ahead = shifted(ahead, 1)
    back = shifted(back, -1)
    dfeed, halo = call(
        dfeed_kernel,
        "dfeed",
        (struct((ch, length + LANE)), struct((ch, LANE))),
        conv_down,
        cot,
        ahead,
        back,
    )
    halo_y = along_chan(halo, 2)
    packs = (pack, along_chan(pack, 1), pack_y, along_chan(pack_y, 1))
    halos = (halo, along_chan(halo, 1), halo_y, along_chan(halo_y, 1))
    feed, hidden = call(
        forward_kernel,
        "forward",
        (struct((ch, length)), struct((LANE, length + LANE), F32)),
        *packs,
        *halos,
    )
    dfeed_y = along_chan(dfeed, 2)
    dfeeds = (dfeed, along_chan(dfeed, 1), dfeed_y, along_chan(dfeed_y, 1))
    grad, weight = call(
        backward_kernel,
        "backward",
        (struct((ch, length)), struct((ch * (KRES + 1), LANE))),
        *packs,
        *halos,
        hidden,
        *dfeeds,
    )
    factor = float(1.0 / np.sqrt(np.float32(clips * times * (length // STRIDE))))
    if (clips, times) == (2, 4):
        cots = jnp.concatenate([quarter, along_group(quarter, 4)])
        cots = jnp.concatenate([cots, along_group(cots, 2)])
        cots = jnp.concatenate([cots, along_group(cots, 1)])
        cots_y = along_chan(cots, 2)
        cots = pl.pallas_call(
            lambda *refs: cot_kernel((0, 4, 2, 6, 1, 5, 3, 7), times * count, *refs),
            out_shape=struct((group * count, 2 * width)),
            scratch_shapes=[pltpu.VMEM((group * count, width), F32)],
            name="cots",
        )(cots, along_chan(cots, 1), cots_y, along_chan(cots_y, 1))
        one, two = feed[:, : length // 2], feed[:, length // 2 :]
        one = jnp.concatenate([one, along_group(one, 4)])
        two = jnp.concatenate([two, along_group(two, 2)])
        one = jnp.concatenate([one, along_group(one, 2)])
        two = jnp.concatenate([two, along_group(two, 1)])
        one_far = along_group(one, 1)
        two_far = along_group(two, 4)
        down = down_half(0, (0, 4, 2, 6, 1, 5, 3, 7), factor, ch, one, one_far, cots, None)
        down = down_half(1, (0, 2, 1, 3, 4, 6, 5, 7), factor, ch, two, two_far, cots, down)
        for step in (4, 2, 1):
            other = along_group(weight, step)
            weight = weight.astype(F32) + other.astype(F32)
            if step > 1:
                weight = weight.astype(BF16)
    else:
        blocks = feed.reshape(ch, STRIDE, count).transpose(1, 0, 2).reshape(STRIDE * ch, count)
        rest = back[ch : ch + width // LANE].reshape(1, width)
        behind = dot(blocks, cot)
        front = dot(blocks, jnp.concatenate([cot[1:], rest]))
        down = jnp.stack([front, behind]) * factor
        down, weight = lax.psum((down, weight.astype(F32)), ("clip", "tm"))
    weight = weight * factor
    return (
        grad.T[None],
        weight[: ch * KRES].reshape(conv_first.shape),
        weight[ch * KRES :].T,
        down.reshape(conv_down.shape),
    )


def solution(mesh):
    return jax.shard_map(
        on_device,
        mesh=mesh,
        in_specs=(
            P("clip", "tm", "chan"),
            P(None, "chan", None),
            P(None, "chan"),
            P(None, "chan", None),
            P("clip", "tm", None),
        ),
        out_specs=(
            P("clip", "tm", "chan"),
            P(None, "chan", None),
            P(None, "chan"),
            P(None, "chan", None),
        ),
        check_vma=False,
    )
```

time: 209 us -> 74.2 us (0.36)
  waiting for transfers between devices: 129 us -> 13.3 us
  blocking collectives: 39.2 us -> 0 us
  Pallas kernels: 0 us -> 22 us
  starting transfers between devices: 6.33 us -> 26.9 us
  between operations: 13.9 us -> 0.91 us
  other arithmetic: 9.89 us -> 2.49 us
  matrix products: 7.15 us -> 0 us
  local copies, waits for them, and re-layouts: 3.4 us -> 8.13 us
    psum x3 -> x0, waiting for transfers between devices: 125 us -> none  [the longest x1 62.3 us: on_device(): lax.psum((first_raw, second_raw, down_raw), ('clip', 'tm'))]
    psum x1 -> x0, blocking collectives: 39.2 us -> none  [on_device(): lax.psum((first_raw, second_raw, down_raw), ('clip', 'tm'))]
    pallas_call x0 -> x7, Pallas kernels: none -> 22 us  [the longest x4 11.7 us: call(): pl.pallas_call(kernel, out_shape=out_shape, scratch_shapes=scratch, name=...]
    ppermute x2 -> x26, starting transfers between devices: 6.21 us -> 26.9 us  [the longest x12 16.9 us: along_group(): lax.ppermute(value, ('clip', 'tm'), [(i, i ^ other) for i in range(count)])]
    ppermute x2 -> x26, waiting for transfers between devices: 3.89 us -> 13.3 us  [the longest x12 9.99 us: along_group(): lax.ppermute(value, ('clip', 'tm'), [(i, i ^ other) for i in range(count)])]
    dot_general x16 -> x0, matrix products: 7.15 us -> none  [the longest x6 2.3 us: contract_cols(): lax.dot_general(left, right, (((1,), (1,)), ((), ())), preferred_element_...]
    unnamed x10 -> x43, local copies, waits for them, and re-layouts: 0.03 us -> 6.84 us
    mul x3 -> x1, other arithmetic: 5.32 us -> 0.02 us  [on_device(): weight = weight * factor]
  transfers between devices with their start and end apart: 5 -> 26, of which waited for: 4 -> 7; matrix products, arithmetic and copies ran while one was open for 3% -> 6% of each run, Pallas kernels for 0% -> 22%
where the time goes in v1:
time: 74.2 us; the launch traced here: 73.6 us
  starting transfers between devices  26.9 us (36%)
  Pallas kernels  22 us (30%)
  waiting for transfers between devices  13.3 us (18%)
  local copies, waits for them, and re-layouts  8.13 us (11%)
  other arithmetic  2.49 us (3%)
  between operations  0.91 us (1%)
    ppermute x12, starting transfers between devices, along_group(): lax.ppermute(value, ('clip', 'tm'), [(i, i ^ other) for i in range(count)])  16.9 us
    pallas_call x4, Pallas kernels, call(): pl.pallas_call(kernel, out_shape=out_shape, scratch_shapes=scratch, name=...  11.7 us
    ppermute x12, waiting for transfers between devices, along_group(): lax.ppermute(value, ('clip', 'tm'), [(i, i ^ other) for i in range(count)])  9.99 us
    pallas_call x2, Pallas kernels, down_half(): pl.pallas_call(body, grid=(1,), in_specs=specs, out_specs=pl.BlockSpec((2...  7.16 us
    unnamed x43, local copies, waits for them, and re-layouts  6.84 us
    ppermute x12, starting transfers between devices, along_chan(): return lax.ppermute(value, 'chan', pairs)  5.27 us
    ppermute x2, starting transfers between devices, shifted(): return lax.ppermute(value, 'tm', route)  4.76 us
    ppermute x12, waiting for transfers between devices, along_chan(): return lax.ppermute(value, 'chan', pairs)  3.26 us
  transfers between devices with their start and end apart: 26, of which 7 were waited for; matrix products, arithmetic and copies ran while one was open for 6% of the time, Pallas kernels for 22%

profile of v1, /device:TPU:0, one launch (start us, length us, event | category | flops | bytes accessed | tf_op | source)
XLA Modules:
  0.0 73.6 jit_solution(2781165852778163763)
XLA Ops:
  0.6 2.1 %prep.1 = (bf16[64,1536]{1,0:T(8,128)(2,1)}, bf16[64,128]{1,0:T(8,128)(2,1)}, bf16[80,128]{1,0:T(8,128)(2,1)}, bf16[32,512]{1,0:T(8,128)(2,1)}) custom-call(bf16[64,1024]{1,0:T(8,128)(2,1)} %bitcast.15, bf16[3,64,128]{2,1,0:T(8,128)(2,1)} %first.1, bf16[64,128]{1,0:T(8,128)(2,1)} %bitcast.17, bf16[128,512]{1,0:T(8,128)(2,1)} %bitcast.13), custom_call_target="tpu_custom_call" | custom-call | tf_op jit(solution)/shard_map/prep/pallas_call | solution.py:264
  2.7 2.9 %collective-permute-start.17 = (bf16[32,512]{1,0:T(8,128)(2,1)}, bf16[32,512]{1,0:T(8,128)(2,1)S(1)}, u32[]{:S(2)}, u32[]{:S(2)}) collective-permute-start(bf16[32,512]{1,0:T(8,128)(2,1)} %get-tuple-element.23), channel_id=1, source_target_pairs={{0,16},{4,20},{8,24},{12,28},{16,0},{20,4},{24,8},{28,12},{1,17},{... | collective-permute-start | bytes 98312 | tf_op jit(solution)/shard_map/ppermute | solution.py:304
  5.7 3.5 %collective-permute-start.3 = (bf16[64,128]{1,0:T(8,128)(2,1)}, bf16[64,128]{1,0:T(8,128)(2,1)S(1)}, u32[]{:S(2)}, u32[]{:S(2)}) collective-permute-start(bf16[64,128]{1,0:T(8,128)(2,1)} %get-tuple-element.15), channel_id=1, source_target_pairs={{0,4},{4,8},{8,12},{1,5},{5,9},{9,13},{2,6},{6,10},{10,14},{3,7},{... | collective-permute-start | bytes 49160 | tf_op jit(solution)/shard_map/ppermute | solution.py:310
  9.2 1.3 %collective-permute-start.4 = (bf16[80,128]{1,0:T(8,128)(2,1)}, bf16[80,128]{1,0:T(8,128)(2,1)S(1)}, u32[]{:S(2)}, u32[]{:S(2)}) collective-permute-start(bf16[80,128]{1,0:T(8,128)(2,1)} %get-tuple-element.16), channel_id=1, source_target_pairs={{4,0},{8,4},{12,8},{5,1},{9,5},{13,9},{6,2},{10,6},{14,10},{7,3},{... | collective-permute-start | bytes 61448 | tf_op jit(solution)/shard_map/ppermute | solution.py:310
  10.5 1.6 %collective-permute-start.1 = (bf16[64,1536]{1,0:T(8,128)(2,1)}, bf16[64,1536]{1,0:T(8,128)(2,1)S(1)}, u32[]{:S(2)}, u32[]{:S(2)}) collective-permute-start(bf16[64,1536]{1,0:T(8,128)(2,1)} %get-tuple-element.14.a0), channel_id=1, source_target_pairs={{0,2},{1,3},{2,0},{3,1},{4,6},{5,7},{6,4},{7,5},{8,10},{9,11},{10,... | collective-permute-start | bytes 589832 | tf_op jit(solution)/shard_map/ppermute | solution.py:299
  12.1 0.8 %pad_maximum_fusion.5 = bf16[64,512]{1,0:T(8,128)(2,1)S(1)} fusion(bf16[32,512]{1,0:T(8,128)(2,1)S(1)} %collective-permute-done.17, bf16[32,512]{1,0:T(8,128)(2,1)} %get-tuple-element.23), kind=kLoop, calls=%fused_computation.8 | loop fusion | flops 131072 | bytes 131072 | tf_op jit(solution)/shard_map/concatenate | solution.py:375
  12.8 3.7 %collective-permute-start.18 = (bf16[64,512]{1,0:T(8,128)(2,1)S(1)}, bf16[64,512]{1,0:T(8,128)(2,1)S(1)}, u32[]{:S(2)}, u32[]{:S(2)}) collective-permute-start(bf16[64,512]{1,0:T(8,128)(2,1)S(1)} %pad_maximum_fusion.5), channel_id=1, source_target_pairs={{0,8},{4,12},{8,0},{12,4},{16,24},{20,28},{24,16},{28,20},{1,9},{5... | collective-permute-start | bytes 196616 | tf_op jit(solution)/shard_map/ppermute | solution.py:304
  16.5 0.8 %constant_dynamic-update-slice_fusion.3 = bf16[256,512]{1,0:T(8,128)(2,1)S(1)} fusion(bf16[32,512]{1,0:T(8,128)(2,1)} %get-tuple-element.23), kind=kLoop, calls=%fused_computation.13 | loop fusion | bytes 65536
  18.5 2.9 %dfeed.1 = (bf16[64,1152]{1,0:T(8,128)(2,1)}, bf16[64,128]{1,0:T(8,128)(2,1)}) custom-call(bf16[16,64,512]{2,1,0:T(8,128)(2,1)} %down.1, bf16[128,512]{1,0:T(8,128)(2,1)} %bitcast.14, bf16[64,128]{1,0:T(8,128)(2,1)} %copy-done.19, bf16[80,128]{1,0:T(8,128)(2,1)} %copy-done.18), custom_call_target="tpu_custom_call" | custom-call | tf_op jit(solution)/shard_map/dfeed/pallas_call | solution.py:264
  21.9 1.5 %collective-permute-start.9 = (bf16[64,1152]{1,0:T(8,128)(2,1)}, bf16[64,1152]{1,0:T(8,128)(2,1)S(1)}, u32[]{:S(2)}, u32[]{:S(2)}) collective-permute-start(bf16[64,1152]{1,0:T(8,128)(2,1)} %get-tuple-element.19.d0), channel_id=1, source_target_pairs={{0,2},{1,3},{2,0},{3,1},{4,6},{5,7},{6,4},{7,5},{8,10},{9,11},{10,... | collective-permute-start | bytes 442376 | tf_op jit(solution)/shard_map/ppermute | solution.py:299
  23.4 0.8 %pad_maximum_fusion.3 = bf16[128,512]{1,0:T(8,128)(2,1)S(1)} fusion(bf16[64,512]{1,0:T(8,128)(2,1)S(1)} %collective-permute-done.18, bf16[32,512]{1,0:T(8,128)(2,1)S(1)} %collective-permute-done.17, bf16[32,512]{1,0:T(8,128)(2,1)} %get-tuple-element.23), kind=kLoop, calls=%fused_computation.3 | loop fusion | flops 393216 | bytes 262144 | tf_op jit(solution)/shard_map/concatenate | solution.py:376
  24.2 1.6 %collective-permute-start.19 = (bf16[128,512]{1,0:T(8,128)(2,1)S(1)}, bf16[128,512]{1,0:T(8,128)(2,1)S(1)}, u32[]{:S(2)}, u32[]{:S(2)}) collective-permute-start(bf16[128,512]{1,0:T(8,128)(2,1)S(1)} %pad_maximum_fusion.3), channel_id=1, source_target_pairs={{0,4},{4,0},{8,12},{12,8},{16,20},{20,16},{24,28},{28,24},{1,5},{5... | collective-permute-start | bytes 393224 | tf_op jit(solution)/shard_map/ppermute | solution.py:304
  26.4 2.1 %collective-permute-done.9.d2 = bf16[64,1152]{1,0:T(8,128)(2,1)S(1)} collective-permute-done((bf16[64,1152]{1,0:T(8,128)(2,1)}, bf16[64,1152]{1,0:T(8,128)(2,1)S(1)}, u32[]{:S(2)}, u32[]{:S(2)}) %collective-permute-start.9) | collective-permute-done | bytes 147488 | tf_op jit(solution)/shard_map/ppermute | solution.py:299
  29.0 0.9 %collective-permute-done.19 = bf16[128,512]{1,0:T(8,128)(2,1)S(1)} collective-permute-done((bf16[128,512]{1,0:T(8,128)(2,1)S(1)}, bf16[128,512]{1,0:T(8,128)(2,1)S(1)}, u32[]{:S(2)}, u32[]{:S(2)}) %collective-permute-start.19) | collective-permute-done | bytes 131104 | tf_op jit(solution)/shard_map/ppermute | solution.py:304
  29.9 1.2 %collective-permute-done.7.h3 = bf16[64,128]{1,0:T(8,128)(2,1)S(1)} collective-permute-done((bf16[64,128]{1,0:T(8,128)(2,1)S(1)}, bf16[64,128]{1,0:T(8,128)(2,1)S(1)}, u32[]{:S(2)}, u32[]{:S(2)}) %collective-permute-start.7) | collective-permute-done | bytes 16416 | tf_op jit(solution)/shard_map/ppermute | solution.py:299
  33.0 2.8 %forward.1 = (bf16[64,1024]{1,0:T(8,128)(2,1)}, f32[128,1152]{1,0:T(8,128)}) custom-call(bf16[64,1536]{1,0:T(8,128)(2,1)} %get-tuple-element.14.a0, bf16[64,1536]{1,0:T(8,128)(2,1)} %copy-done.3, bf16[64,1536]{1,0:T(8,128)(2,1)} %copy-done.2, bf16[64,1536]{1,0:T(8,128)(2,1)} %copy-done.4, bf16[64,128]{1,0:T(8,128)(2,1)} %get-tuple-element.17.h0, ...), custom_call_target="tpu_custom_call" | custom-call | tf_op jit(solution)/shard_map/forward/pallas_call | solution.py:264
  36.6 3.8 %backward.1 = (bf16[64,1024]{1,0:T(8,128)(2,1)}, bf16[256,128]{1,0:T(8,128)(2,1)}) custom-call(bf16[64,1536]{1,0:T(8,128)(2,1)} %get-tuple-element.14.a0, bf16[64,1536]{1,0:T(8,128)(2,1)} %copy-done.3, bf16[64,1536]{1,0:T(8,128)(2,1)} %copy-done.2, bf16[64,1536]{1,0:T(8,128)(2,1)} %copy-done.4, bf16[64,128]{1,0:T(8,128)(2,1)} %get-tuple-element.17.h0, ...), custom_call_target="tpu_custom_call" | custom-call | tf_op jit(solution)/shard_map/backward/pallas_call | solution.py:264
  40.9 1.6 %collective-permute-start.23 = (bf16[64,512]{1,0:T(8,128)(2,1)S(1)}, bf16[64,512]{1,0:T(8,128)(2,1)S(1)}, u32[]{:S(2)}, u32[]{:S(2)}) collective-permute-start(bf16[64,512]{1,0:T(8,128)(2,1)S(1)} %get-tuple-element.24), channel_id=1, source_target_pairs={{0,16},{4,20},{8,24},{12,28},{16,0},{20,4},{24,8},{28,12},{1,17},{... | collective-permute-start | bytes 196616 | tf_op jit(solution)/shard_map/ppermute | solution.py:304
  42.5 0.7 collective-permute-start.14
  43.2 2.0 %collective-permute-done.11 = bf16[256,128]{1,0:T(8,128)(2,1)S(1)} collective-permute-done((bf16[256,128]{1,0:T(8,128)(2,1)}, bf16[256,128]{1,0:T(8,128)(2,1)S(1)}, u32[]{:S(2)}, u32[]{:S(2)}) %collective-permute-start.11) | collective-permute-done | bytes 65568 | tf_op jit(solution)/shard_map/ppermute | solution.py:304
  45.2 0.9 %add_convert_fusion.1 = bf16[256,128]{1,0:T(8,128)(2,1)S(1)} fusion(bf16[256,128]{1,0:T(8,128)(2,1)S(1)} %collective-permute-done.11, bf16[256,128]{1,0:T(8,128)(2,1)} %get-tuple-element.21), kind=kLoop, calls=%fused_computation.7 | loop fusion | flops 131072 | bytes 196608 | tf_op jit(solution)/shard_map/convert_element_type | solution.py:398
  46.1 0.7 %collective-permute-start.12 = (bf16[256,128]{1,0:T(8,128)(2,1)S(1)}, bf16[256,128]{1,0:T(8,128)(2,1)S(1)}, u32[]{:S(2)}, u32[]{:S(2)}) collective-permute-start(bf16[256,128]{1,0:T(8,128)(2,1)S(1)} %add_convert_fusion.1), channel_id=1, source_target_pairs={{0,8},{4,12},{8,0},{12,4},{16,24},{20,28},{24,16},{28,20},{1,9},{5... | collective-permute-start | bytes 196616 | tf_op jit(solution)/shard_map/ppermute | solution.py:304
  46.8 2.3 %collective-permute-start.24 = (bf16[128,512]{1,0:T(8,128)(2,1)S(1)}, bf16[128,512]{1,0:T(8,128)(2,1)S(1)}, u32[]{:S(2)}, u32[]{:S(2)}) collective-permute-start(bf16[128,512]{1,0:T(8,128)(2,1)S(1)} %pad_maximum_fusion.4), channel_id=1, source_target_pairs={{0,8},{4,12},{8,0},{12,4},{16,24},{20,28},{24,16},{28,20},{1,9},{5... | collective-permute-start | bytes 393224 | tf_op jit(solution)/shard_map/ppermute | solution.py:304
  49.2 1.6 %collective-permute-start.15 = (bf16[128,512]{1,0:T(8,128)(2,1)S(1)}, bf16[128,512]{1,0:T(8,128)(2,1)S(1)}, u32[]{:S(2)}, u32[]{:S(2)}) collective-permute-start(bf16[128,512]{1,0:T(8,128)(2,1)S(1)} %pad_maximum_fusion.2), channel_id=1, source_target_pairs={{0,4},{4,0},{8,12},{12,8},{16,20},{20,16},{24,28},{28,24},{1,5},{5... | collective-permute-start | bytes 393224 | tf_op jit(solution)/shard_map/ppermute | solution.py:304
  50.8 2.8 %collective-permute-done.12 = bf16[256,128]{1,0:T(8,128)(2,1)S(1)} collective-permute-done((bf16[256,128]{1,0:T(8,128)(2,1)S(1)}, bf16[256,128]{1,0:T(8,128)(2,1)S(1)}, u32[]{:S(2)}, u32[]{:S(2)}) %collective-permute-start.12) | collective-permute-done | bytes 65568 | tf_op jit(solution)/shard_map/ppermute | solution.py:304
  53.7 3.5 %collective-permute-done.15 = bf16[128,512]{1,0:T(8,128)(2,1)S(1)} collective-permute-done((bf16[128,512]{1,0:T(8,128)(2,1)S(1)}, bf16[128,512]{1,0:T(8,128)(2,1)S(1)}, u32[]{:S(2)}, u32[]{:S(2)}) %collective-permute-start.15) | collective-permute-done | bytes 131104 | tf_op jit(solution)/shard_map/ppermute | solution.py:304
  57.3 1.0 %collective-permute-start.16 = (bf16[256,512]{1,0:T(8,128)(2,1)S(1)}, bf16[256,512]{1,0:T(8,128)(2,1)S(1)}, u32[]{:S(2)}, u32[]{:S(2)}) collective-permute-start(bf16[256,512]{1,0:T(8,128)(2,1)S(1)} %pad_maximum_fusion.n), channel_id=1, source_target_pairs={{0,16},{4,20},{8,24},{12,28},{16,0},{20,4},{24,8},{28,12},{1,17},{... | collective-permute-start | bytes 786440 | tf_op jit(solution)/shard_map/ppermute | solution.py:304
  61.1 3.1 %cots.1.refs_2_.c = bf16[1024,1024]{1,0:T(8,128)(2,1)} custom-call(bf16[256,512]{1,0:T(8,128)(2,1)} %copy-done.5, bf16[256,512]{1,0:T(8,128)(2,1)} %copy-done.7, bf16[256,512]{1,0:T(8,128)(2,1)} %copy-done.6, bf16[256,512]{1,0:T(8,128)(2,1)} %copy-done.8), custom_call_target="tpu_custom_call" | custom-call | tf_op jit(solution)/shard_map/cots/pallas_call | solution.py:379
  64.2 0.8 %collective-permute-done.25.refs_1_ = bf16[256,512]{1,0:T(8,128)(2,1)S(1)} collective-permute-done((bf16[256,512]{1,0:T(8,128)(2,1)S(1)}, bf16[256,512]{1,0:T(8,128)(2,1)S(1)}, u32[]{:S(2)}, u32[]{:S(2)}) %collective-permute-start.25) | collective-permute-done | bytes 262176 | tf_op jit(solution)/shard_map/ppermute | solution.py:304
  65.0 0.7 copy-done.9
  65.8 3.6 %down0.1.p = f32[2,8,64,512]{3,2,1,0:T(8,128)} custom-call(bf16[256,512]{1,0:T(8,128)(2,1)} %copy-done, bf16[256,512]{1,0:T(8,128)(2,1)} %copy-done.9, bf16[1024,1024]{1,0:T(8,128)(2,1)} %cots.1.refs_2_.c), custom_call_target="tpu_custom_call" | custom-call | tf_op jit(solution)/shard_map/down0/pallas_call | solution.py:285
  70.1 3.6 %down1.1 = f32[2,8,64,512]{3,2,1,0:T(8,128)} custom-call(bf16[256,512]{1,0:T(8,128)(2,1)} %copy-done.1, bf16[256,512]{1,0:T(8,128)(2,1)} %copy-done.10, bf16[1024,1024]{1,0:T(8,128)(2,1)} %cots.1.refs_2_.c, f32[2,8,64,512]{3,2,1,0:T(8,128)} %down0.1.p), custom_call_target="tpu_custom_call", output_to_operand_aliasing={{}: (3, {})} | custom-call | tf_op jit(solution)/shard_map/down1/pallas_call | solution.py:285
  (83 shorter events, 9.6 us)
Async XLA Ops:
  2.7 9.3 %collective-permute-start.17 = (bf16[32,512]{1,0:T(8,128)(2,1)}, bf16[32,512]{1,0:T(8,128)(2,1)S(1)}, u32[]{:S(2)}, u32[]{:S(2)}) collective-permute-start(bf16[32,512]{1,0:T(8,128)(2,1)} %get-tuple-element.23), channel_id=1, source_target_pairs={{0,16},{4,20},{8,24},{12,28},{16,0},{20,4},{24,8},{28,12},{1,17},{... | collective-permute-start | bytes 98312 | tf_op jit(solution)/shard_map/ppermute | solution.py:304
  5.7 11.6 %collective-permute-start.3 = (bf16[64,128]{1,0:T(8,128)(2,1)}, bf16[64,128]{1,0:T(8,128)(2,1)S(1)}, u32[]{:S(2)}, u32[]{:S(2)}) collective-permute-start(bf16[64,128]{1,0:T(8,128)(2,1)} %get-tuple-element.15), channel_id=1, source_target_pairs={{0,4},{4,8},{8,12},{1,5},{5,9},{9,13},{2,6},{6,10},{10,14},{3,7},{... | collective-permute-start | bytes 49160 | tf_op jit(solution)/shard_map/ppermute | solution.py:310
  9.2 8.1 %collective-permute-start.4 = (bf16[80,128]{1,0:T(8,128)(2,1)}, bf16[80,128]{1,0:T(8,128)(2,1)S(1)}, u32[]{:S(2)}, u32[]{:S(2)}) collective-permute-start(bf16[80,128]{1,0:T(8,128)(2,1)} %get-tuple-element.16), channel_id=1, source_target_pairs={{4,0},{8,4},{12,8},{5,1},{9,5},{13,9},{6,2},{10,6},{14,10},{7,3},{... | collective-permute-start | bytes 61448 | tf_op jit(solution)/shard_map/ppermute | solution.py:310
  10.5 18.0 %collective-permute-start.1 = (bf16[64,1536]{1,0:T(8,128)(2,1)}, bf16[64,1536]{1,0:T(8,128)(2,1)S(1)}, u32[]{:S(2)}, u32[]{:S(2)}) collective-permute-start(bf16[64,1536]{1,0:T(8,128)(2,1)} %get-tuple-element.14.a0), channel_id=1, source_target_pairs={{0,2},{1,3},{2,0},{3,1},{4,6},{5,7},{6,4},{7,5},{8,10},{9,11},{10,... | collective-permute-start | bytes 589832 | tf_op jit(solution)/shard_map/ppermute | solution.py:299
  12.8 10.6 %collective-permute-start.18 = (bf16[64,512]{1,0:T(8,128)(2,1)S(1)}, bf16[64,512]{1,0:T(8,128)(2,1)S(1)}, u32[]{:S(2)}, u32[]{:S(2)}) collective-permute-start(bf16[64,512]{1,0:T(8,128)(2,1)S(1)} %pad_maximum_fusion.5), channel_id=1, source_target_pairs={{0,8},{4,12},{8,0},{12,4},{16,24},{20,28},{24,16},{28,20},{1,9},{5... | collective-permute-start | bytes 196616 | tf_op jit(solution)/shard_map/ppermute | solution.py:304
  21.4 4.4 %collective-permute-start.6 = (bf16[64,128]{1,0:T(8,128)(2,1)}, bf16[64,128]{1,0:T(8,128)(2,1)S(1)}, u32[]{:S(2)}, u32[]{:S(2)}) collective-permute-start(bf16[64,128]{1,0:T(8,128)(2,1)} %get-tuple-element.17.h0), channel_id=1, source_target_pairs={{0,2},{1,3},{2,0},{3,1},{4,6},{5,7},{6,4},{7,5},{8,10},{9,11},{10,... | collective-permute-start | bytes 49160 | tf_op jit(solution)/shard_map/ppermute | solution.py:299
  21.9 4.0 %collective-permute-start.5 = (bf16[64,128]{1,0:T(8,128)(2,1)}, bf16[64,128]{1,0:T(8,128)(2,1)S(1)}, u32[]{:S(2)}, u32[]{:S(2)}) collective-permute-start(bf16[64,128]{1,0:T(8,128)(2,1)} %get-tuple-element.17.h0), channel_id=1, source_target_pairs={{0,1},{1,0},{2,3},{3,2},{4,5},{5,4},{6,7},{7,6},{8,9},{9,8},{10,11... | collective-permute-start | bytes 49160 | tf_op jit(solution)/shard_map/ppermute | solution.py:299
  21.9 6.6 %collective-permute-start.9 = (bf16[64,1152]{1,0:T(8,128)(2,1)}, bf16[64,1152]{1,0:T(8,128)(2,1)S(1)}, u32[]{:S(2)}, u32[]{:S(2)}) collective-permute-start(bf16[64,1152]{1,0:T(8,128)(2,1)} %get-tuple-element.19.d0), channel_id=1, source_target_pairs={{0,2},{1,3},{2,0},{3,1},{4,6},{5,7},{6,4},{7,5},{8,10},{9,11},{10,... | collective-permute-start | bytes 442376 | tf_op jit(solution)/shard_map/ppermute | solution.py:299
  24.2 5.7 %collective-permute-start.19 = (bf16[128,512]{1,0:T(8,128)(2,1)S(1)}, bf16[128,512]{1,0:T(8,128)(2,1)S(1)}, u32[]{:S(2)}, u32[]{:S(2)}) collective-permute-start(bf16[128,512]{1,0:T(8,128)(2,1)S(1)} %pad_maximum_fusion.3), channel_id=1, source_target_pairs={{0,4},{4,0},{8,12},{12,8},{16,20},{20,16},{24,28},{28,24},{1,5},{5... | collective-permute-start | bytes 393224 | tf_op jit(solution)/shard_map/ppermute | solution.py:304
  25.8 5.9 %copy-start.15 = (bf16[64,128]{1,0:T(8,128)(2,1)}, bf16[64,128]{1,0:T(8,128)(2,1)S(1)}, u32[]{:S(2)}) copy-start(bf16[64,128]{1,0:T(8,128)(2,1)S(1)} %collective-permute-done.6.h2) | copy-start | bytes 49156
  25.8 5.8 %collective-permute-start = (bf16[64,1536]{1,0:T(8,128)(2,1)}, bf16[64,1536]{1,0:T(8,128)(2,1)S(1)}, u32[]{:S(2)}, u32[]{:S(2)}) collective-permute-start(bf16[64,1536]{1,0:T(8,128)(2,1)} %get-tuple-element.14.a0), channel_id=1, source_target_pairs={{0,1},{1,0},{2,3},{3,2},{4,5},{5,4},{6,7},{7,6},{8,9},{9,8},{10,11... | collective-permute-start | bytes 589832 | tf_op jit(solution)/shard_map/ppermute | solution.py:299
  25.9 9.9 %collective-permute-start.8 = (bf16[64,1152]{1,0:T(8,128)(2,1)}, bf16[64,1152]{1,0:T(8,128)(2,1)S(1)}, u32[]{:S(2)}, u32[]{:S(2)}) collective-permute-start(bf16[64,1152]{1,0:T(8,128)(2,1)} %get-tuple-element.19.d0), channel_id=1, source_target_pairs={{0,1},{1,0},{2,3},{3,2},{4,5},{5,4},{6,7},{7,6},{8,9},{9,8},{10,11... | collective-permute-start | bytes 442376 | tf_op jit(solution)/shard_map/ppermute | solution.py:299
  28.5 7.4 %copy-start.11 = (bf16[64,1152]{1,0:T(8,128)(2,1)}, bf16[64,1152]{1,0:T(8,128)(2,1)S(1)}, u32[]{:S(2)}) copy-start(bf16[64,1152]{1,0:T(8,128)(2,1)S(1)} %collective-permute-done.9.d2) | copy-start | bytes 442372
  28.5 7.4 %collective-permute-start.10 = (bf16[64,1152]{1,0:T(8,128)(2,1)S(1)}, bf16[64,1152]{1,0:T(8,128)(2,1)S(1)}, u32[]{:S(2)}, u32[]{:S(2)}) collective-permute-start(bf16[64,1152]{1,0:T(8,128)(2,1)S(1)} %collective-permute-done.9.d2), channel_id=1, source_target_pairs={{0,1},{1,0},{2,3},{3,2},{4,5},{5,4},{6,7},{7,6},{8,9},{9,8},{10,11... | collective-permute-start | bytes 442376 | tf_op jit(solution)/shard_map/ppermute | solution.py:299
  28.5 3.2 %collective-permute-start.2 = (bf16[64,1536]{1,0:T(8,128)(2,1)S(1)}, bf16[64,1536]{1,0:T(8,128)(2,1)S(1)}, u32[]{:S(2)}, u32[]{:S(2)}) collective-permute-start(bf16[64,1536]{1,0:T(8,128)(2,1)S(1)} %collective-permute-done.1.a2), channel_id=1, source_target_pairs={{0,1},{1,0},{2,3},{3,2},{4,5},{5,4},{6,7},{7,6},{8,9},{9,8},{10,11... | collective-permute-start | bytes 589832 | tf_op jit(solution)/shard_map/ppermute | solution.py:299
  29.9 1.2 %collective-permute-start.7 = (bf16[64,128]{1,0:T(8,128)(2,1)S(1)}, bf16[64,128]{1,0:T(8,128)(2,1)S(1)}, u32[]{:S(2)}, u32[]{:S(2)}) collective-permute-start(bf16[64,128]{1,0:T(8,128)(2,1)S(1)} %collective-permute-done.6.h2), channel_id=1, source_target_pairs={{0,1},{1,0},{2,3},{3,2},{4,5},{5,4},{6,7},{7,6},{8,9},{9,8},{10,11... | collective-permute-start | bytes 49160 | tf_op jit(solution)/shard_map/ppermute | solution.py:299
  29.9 29.8 %copy-start.5 = (bf16[256,512]{1,0:T(8,128)(2,1)}, bf16[256,512]{1,0:T(8,128)(2,1)S(1)}, u32[]{:S(2)}) copy-start(bf16[256,512]{1,0:T(8,128)(2,1)S(1)} %constant_dynamic-update-slice_fusion.refs_0_) | copy-start | bytes 786436
  31.1 19.7 %collective-permute-start.21 = (bf16[256,512]{1,0:T(8,128)(2,1)S(1)}, bf16[256,512]{1,0:T(8,128)(2,1)S(1)}, u32[]{:S(2)}, u32[]{:S(2)}) collective-permute-start(bf16[256,512]{1,0:T(8,128)(2,1)S(1)} %constant_dynamic-update-slice_fusion.refs_0_), channel_id=1, source_target_pairs={{0,2},{1,3},{2,0},{3,1},{4,6},{5,7},{6,4},{7,5},{8,10},{9,11},{10,... | collective-permute-start | bytes 786440 | tf_op jit(solution)/shard_map/ppermute | solution.py:299
  31.7 28.0 %collective-permute-start.20 = (bf16[256,512]{1,0:T(8,128)(2,1)S(1)}, bf16[256,512]{1,0:T(8,128)(2,1)S(1)}, u32[]{:S(2)}, u32[]{:S(2)}) collective-permute-start(bf16[256,512]{1,0:T(8,128)(2,1)S(1)} %constant_dynamic-update-slice_fusion.refs_0_), channel_id=1, source_target_pairs={{0,1},{1,0},{2,3},{3,2},{4,5},{5,4},{6,7},{7,6},{8,9},{9,8},{10,11... | collective-permute-start | bytes 786440 | tf_op jit(solution)/shard_map/ppermute | solution.py:299
  40.4 4.8 %collective-permute-start.11 = (bf16[256,128]{1,0:T(8,128)(2,1)}, bf16[256,128]{1,0:T(8,128)(2,1)S(1)}, u32[]{:S(2)}, u32[]{:S(2)}) collective-permute-start(bf16[256,128]{1,0:T(8,128)(2,1)} %get-tuple-element.21), channel_id=1, source_target_pairs={{0,16},{4,20},{8,24},{12,28},{16,0},{20,4},{24,8},{28,12},{1,17},{... | collective-permute-start | bytes 196616 | tf_op jit(solution)/shard_map/ppermute | solution.py:304
  40.9 5.9 %collective-permute-start.23 = (bf16[64,512]{1,0:T(8,128)(2,1)S(1)}, bf16[64,512]{1,0:T(8,128)(2,1)S(1)}, u32[]{:S(2)}, u32[]{:S(2)}) collective-permute-start(bf16[64,512]{1,0:T(8,128)(2,1)S(1)} %get-tuple-element.24), channel_id=1, source_target_pairs={{0,16},{4,20},{8,24},{12,28},{16,0},{20,4},{24,8},{28,12},{1,17},{... | collective-permute-start | bytes 196616 | tf_op jit(solution)/shard_map/ppermute | solution.py:304
  42.5 6.7 %collective-permute-start.14 = (bf16[64,512]{1,0:T(8,128)(2,1)S(1)}, bf16[64,512]{1,0:T(8,128)(2,1)S(1)}, u32[]{:S(2)}, u32[]{:S(2)}) collective-permute-start(bf16[64,512]{1,0:T(8,128)(2,1)S(1)} %get-tuple-element.25), channel_id=1, source_target_pairs={{0,8},{4,12},{8,0},{12,4},{16,24},{20,28},{24,16},{28,20},{1,9},{5... | collective-permute-start | bytes 196616 | tf_op jit(solution)/shard_map/ppermute | solution.py:304
  46.1 7.5 %collective-permute-start.12 = (bf16[256,128]{1,0:T(8,128)(2,1)S(1)}, bf16[256,128]{1,0:T(8,128)(2,1)S(1)}, u32[]{:S(2)}, u32[]{:S(2)}) collective-permute-start(bf16[256,128]{1,0:T(8,128)(2,1)S(1)} %add_convert_fusion.1), channel_id=1, source_target_pairs={{0,8},{4,12},{8,0},{12,4},{16,24},{20,28},{24,16},{28,20},{1,9},{5... | collective-permute-start | bytes 196616 | tf_op jit(solution)/shard_map/ppermute | solution.py:304
  46.8 11.4 %collective-permute-start.24 = (bf16[128,512]{1,0:T(8,128)(2,1)S(1)}, bf16[128,512]{1,0:T(8,128)(2,1)S(1)}, u32[]{:S(2)}, u32[]{:S(2)}) collective-permute-start(bf16[128,512]{1,0:T(8,128)(2,1)S(1)} %pad_maximum_fusion.4), channel_id=1, source_target_pairs={{0,8},{4,12},{8,0},{12,4},{16,24},{20,28},{24,16},{28,20},{1,9},{5... | collective-permute-start | bytes 393224 | tf_op jit(solution)/shard_map/ppermute | solution.py:304
  49.2 8.1 %collective-permute-start.15 = (bf16[128,512]{1,0:T(8,128)(2,1)S(1)}, bf16[128,512]{1,0:T(8,128)(2,1)S(1)}, u32[]{:S(2)}, u32[]{:S(2)}) collective-permute-start(bf16[128,512]{1,0:T(8,128)(2,1)S(1)} %pad_maximum_fusion.2), channel_id=1, source_target_pairs={{0,4},{4,0},{8,12},{12,8},{16,20},{20,16},{24,28},{28,24},{1,5},{5... | collective-permute-start | bytes 393224 | tf_op jit(solution)/shard_map/ppermute | solution.py:304
  50.8 8.9 %copy-start.6 = (bf16[256,512]{1,0:T(8,128)(2,1)}, bf16[256,512]{1,0:T(8,128)(2,1)S(1)}, u32[]{:S(2)}) copy-start(bf16[256,512]{1,0:T(8,128)(2,1)S(1)} %collective-permute-done.21.refs_2_) | copy-start | bytes 786436
  50.8 8.9 %collective-permute-start.22 = (bf16[256,512]{1,0:T(8,128)(2,1)S(1)}, bf16[256,512]{1,0:T(8,128)(2,1)S(1)}, u32[]{:S(2)}, u32[]{:S(2)}) collective-permute-start(bf16[256,512]{1,0:T(8,128)(2,1)S(1)} %collective-permute-done.21.refs_2_), channel_id=1, source_target_pairs={{0,1},{1,0},{2,3},{3,2},{4,5},{5,4},{6,7},{7,6},{8,9},{9,8},{10,11... | collective-permute-start | bytes 786440 | tf_op jit(solution)/shard_map/ppermute | solution.py:299
  53.7 4.7 %collective-permute-start.13 = (bf16[256,128]{1,0:T(8,128)(2,1)S(1)}, bf16[256,128]{1,0:T(8,128)(2,1)S(1)}, u32[]{:S(2)}, u32[]{:S(2)}) collective-permute-start(bf16[256,128]{1,0:T(8,128)(2,1)S(1)} %add_convert_fusion), channel_id=1, source_target_pairs={{0,4},{4,0},{8,12},{12,8},{16,20},{20,16},{24,28},{28,24},{1,5},{5... | collective-permute-start | bytes 196616 | tf_op jit(solution)/shard_map/ppermute | solution.py:304
  57.3 7.0 %copy-start.1 = (bf16[256,512]{1,0:T(8,128)(2,1)}, bf16[256,512]{1,0:T(8,128)(2,1)S(1)}, u32[]{:S(2)}) copy-start(bf16[256,512]{1,0:T(8,128)(2,1)S(1)} %pad_maximum_fusion.n) | copy-start | bytes 786436
  57.3 12.1 %collective-permute-start.16 = (bf16[256,512]{1,0:T(8,128)(2,1)S(1)}, bf16[256,512]{1,0:T(8,128)(2,1)S(1)}, u32[]{:S(2)}, u32[]{:S(2)}) collective-permute-start(bf16[256,512]{1,0:T(8,128)(2,1)S(1)} %pad_maximum_fusion.n), channel_id=1, source_target_pairs={{0,16},{4,20},{8,24},{12,28},{16,0},{20,4},{24,8},{28,12},{1,17},{... | collective-permute-start | bytes 786440 | tf_op jit(solution)/shard_map/ppermute | solution.py:304
  58.3 6.7 %copy-start = (bf16[256,512]{1,0:T(8,128)(2,1)}, bf16[256,512]{1,0:T(8,128)(2,1)S(1)}, u32[]{:S(2)}) copy-start(bf16[256,512]{1,0:T(8,128)(2,1)S(1)} %pad_maximum_fusion.1.refs_0_) | copy-start | bytes 786436
  58.3 6.7 %collective-permute-start.25 = (bf16[256,512]{1,0:T(8,128)(2,1)S(1)}, bf16[256,512]{1,0:T(8,128)(2,1)S(1)}, u32[]{:S(2)}, u32[]{:S(2)}) collective-permute-start(bf16[256,512]{1,0:T(8,128)(2,1)S(1)} %pad_maximum_fusion.1.refs_0_), channel_id=1, source_target_pairs={{0,4},{4,0},{8,12},{12,8},{16,20},{20,16},{24,28},{28,24},{1,5},{5... | collective-permute-start | bytes 786440 | tf_op jit(solution)/shard_map/ppermute | solution.py:304
  (14 other events, 21.5 us)

commit v2 on v1

v2 whole, which is shorter than its diff:
```python
import jax
import jax.numpy as jnp
import numpy as np
from jax import lax
from jax.experimental import pallas as pl
from jax.experimental.pallas import tpu as pltpu
from jax.sharding import PartitionSpec as P

KRES = 3
STRIDE = 8
LANE = 128
F32 = jnp.float32
BF16 = jnp.bfloat16


def dot(left, right, dims=((1,), (0,))):
    return lax.dot_general(left, right, (dims, ((), ())), preferred_element_type=F32)


def elu(value):
    return jnp.where(value > 0, value, jnp.exp(jnp.minimum(value, 0.0)) - 1.0)


def slope(value):
    return jnp.where(value > 0, 1.0, jnp.exp(jnp.minimum(value, 0.0)))


def lane_of(shape):
    return lax.broadcasted_iota(jnp.int32, shape, 1)


def roll(value, shift):
    return pltpu.roll(value, shift % value.shape[1], 1)


def swap_chunks(blocks):
    chunk = lane_of(blocks[0].shape) // 16
    blocks = list(blocks)
    for s in (1, 2, 4):
        low = (chunk & s) == 0
        new = list(blocks)
        for i in range(8):
            if i & s == 0:
                a, b = blocks[i], blocks[i | s]
                new[i] = jnp.where(low, a, roll(b, 16 * s))
                new[i | s] = jnp.where(low, roll(a, -16 * s), b)
        blocks = new
    return blocks


def interleaver():
    row = lax.broadcasted_iota(jnp.int32, (LANE, LANE), 0)
    col = lax.broadcasted_iota(jnp.int32, (LANE, LANE), 1)
    return jnp.where(col == 16 * (row % 8) + row // 8, 1.0, 0.0).astype(BF16)


def to_phase(blocks):
    rows = blocks[0].shape[0]
    mixed = dot(jnp.concatenate(blocks, axis=0), interleaver())
    return swap_chunks([mixed[rows * b : rows * (b + 1)] for b in range(8)])


def to_time(blocks):
    rows = blocks[0].shape[0]
    mixed = jnp.concatenate(swap_chunks(blocks), axis=0).astype(BF16)
    out = dot(mixed, interleaver(), ((1,), (1,)))
    return [out[rows * b : rows * (b + 1)] for b in range(8)]


def cut(value, n=8):
    return [value[:, LANE * k : LANE * (k + 1)] for k in range(n)]


def pack_kernel(sig, first, second, cot, down, pack, edge):
    ch, length = sig.shape
    blocks = cut(sig[...])
    for k, block in enumerate(to_phase(blocks)):
        pack[:, LANE * k : LANE * (k + 1)] = block.astype(BF16)
    for k in range(KRES):
        pack[:, length + LANE * k : length + LANE * (k + 1)] = first[k]
    start = length + LANE * (KRES + 1)
    pack[:, start - LANE : start] = second[...]
    lane = lane_of((ch, LANE))
    share = roll(blocks[0].astype(F32), 2)
    upstream = cot[...]
    for k in range(8):
        front = dot(down[k], upstream, ((1,), (1,)))
        back = dot(down[k + 8], upstream, ((1,), (1,)))
        share = jnp.where(lane == 4 + k, roll(front, 4 + k), share)
        if k < 2:
            share = jnp.where(lane == 12 + k, roll(front, 11 + k) + roll(back, 12 + k), share)
        main = jnp.where(lane == LANE - 1, 0.0, roll(front, -1)) + back
        pack[:, start + LANE * k : start + LANE * (k + 1)] = main.astype(BF16)
    edge[:ch, :] = roll(blocks[7].astype(F32), 2).astype(BF16)
    edge[ch:, :] = share.astype(BF16)


def merge_kernel(even, odd, halo):
    ch = halo.shape[0]
    low = lax.axis_index("tm") % 2 == 0
    lane = lane_of((ch, LANE))
    even, odd = even[...].astype(F32), odd[...].astype(F32)
    ahead = jnp.where(low, odd[:ch], even[:ch])
    back = jnp.where(low, even[ch:], odd[ch:])
    near = jnp.where(lane < 2, ahead, jnp.where(lane < 14, back, 0.0))
    halo[...] = near.astype(BF16)


def join_kernel(pack, halo, pack_y, halo_y, pair):
    ch, width = pack.shape
    pair[:ch, :width] = pack[...]
    pair[:ch, width:] = halo[...]
    pair[ch:, :width] = pack_y[...]
    pair[ch:, width:] = halo_y[...]


def forward_kernel(pair, other, one, two, hidden):
    length = 2 * one.shape[1]
    ch = one.shape[0]
    taps = length + KRES * LANE
    halo = taps + LANE + length
    pieces = [jnp.concatenate([p[:, :length], p[:, halo:]], axis=1) for p in (pair, other)]
    act = elu(jnp.concatenate(pieces, axis=0).astype(F32)).astype(BF16)
    weights = jnp.concatenate([p[:, length:taps] for p in (pair, other)], axis=0)
    part = dot(weights, act, ((0,), (0,)))
    p0, p1, p2 = [cut(part[LANE * k : LANE * (k + 1)], 9) for k in range(KRES)]
    lane = lane_of((LANE, LANE))
    wrap6, wrap7, twice7 = roll(p0[6], 1), roll(p1[7], 1), roll(p0[7], 1)
    out = [None] * 9
    out[0] = (
        jnp.where(lane == 0, p0[8], wrap6) + jnp.where(lane == 0, roll(p1[8], -1), wrap7) + p2[0]
    )
    out[1] = jnp.where(lane == 0, roll(p0[8], -1), twice7) + p1[0] + p2[1]
    for k in range(2, 8):
        out[k] = p0[k - 2] + p1[k - 1] + p2[k]
    late = roll(p2[8], -2)
    out[8] = jnp.where(
        lane == 0,
        wrap6 + wrap7 + late,
        jnp.where(lane == 1, roll(twice7, 1) + roll(p1[8], -1) + late, 0.0),
    )
    for k in range(9):
        hidden[:, LANE * k : LANE * (k + 1)] = out[k]
    inner = elu(jnp.concatenate(out[:8], axis=1)).astype(BF16)
    resid = pair[:ch, :length].astype(F32) + dot(pair[:ch, taps : taps + LANE], inner)
    feed = elu(resid).astype(BF16)
    one[...] = feed[:, : length // 2]
    two[...] = feed[:, length // 2 :]


def backward_kernel(pair, other, hidden, grad, weight):
    ch, length = grad.shape
    taps = length + KRES * LANE
    start = taps + LANE
    halo = start + length
    last = lane_of((2 * ch, LANE)) == LANE - 1
    behind = lane_of((2 * ch, LANE)) < 2
    hid = hidden[...]
    decay = jnp.exp(jnp.minimum(hid, 0.0))
    inner = jnp.where(hid > 0, hid, decay - 1.0).astype(BF16)
    hid_slope = jnp.where(hid > 0, 1.0, decay)
    mix = jnp.concatenate([p[:, taps:start] for p in (pair, other)], axis=0)
    bent = dot(mix, inner)
    own = None
    rounded = []
    for i, p in enumerate((pair, other)):
        near = p[:, halo:].astype(F32)
        lead = jnp.concatenate([p[:, :length].astype(F32), roll(near, -2)], axis=1)
        resid = lead + bent[2 * ch * i : 2 * ch * (i + 1)]
        dfeed = cut(p[:, start:halo].astype(F32))
        dfeed = [d + jnp.where(last, roll(near, LANE - 5 - k), 0.0) for k, d in enumerate(dfeed)]
        dfeed.append(jnp.where(behind, roll(near, -12), 0.0))
        dres = jnp.concatenate(dfeed, axis=1) * slope(resid)
        if i == 0:
            own = dres[:ch]
        rounded.append(dres.astype(BF16))
    dres16 = jnp.concatenate(rounded, axis=0)
    dinner = dot(mix, dres16, ((0,), (0,)))
    dhid = (dinner * hid_slope).astype(BF16)
    second = dot(rounded[0][:ch, :length], inner[:, :length], ((1,), (1,)))
    weight[:, LANE * KRES :] = second.astype(BF16)
    raw = pair[:ch, :length].astype(F32)
    raw_decay = jnp.exp(jnp.minimum(raw, 0.0))
    act = cut(jnp.where(raw > 0, raw, raw_decay - 1.0))
    edge = elu(pair[:ch, halo:].astype(F32))
    lane = lane_of((ch, LANE))
    before1 = jnp.where(lane == 0, roll(edge, -1), roll(act[7], 1))
    before2 = jnp.where(lane == 0, edge, roll(act[6], 1))
    act = [v.astype(BF16) for v in [before2, before1] + act]
    stack = jnp.concatenate(
        [jnp.concatenate(act[k : k + 8], axis=1) for k in range(KRES)], axis=0
    )
    first = dot(stack, dhid[:, :length], ((1,), (1,)))
    for k in range(KRES):
        weight[:, LANE * k : LANE * (k + 1)] = first[ch * k : ch * (k + 1)].astype(BF16)
    taps_own = jnp.concatenate(
        [pair[:ch, length + LANE * k : length + LANE * (k + 1)] for k in range(KRES)], axis=0
    )
    spread = dot(taps_own, dhid)
    q0, q1, q2 = [cut(spread[ch * k : ch * (k + 1)], 9) for k in range(KRES)]
    last = lane == LANE - 1
    q1next = jnp.where(last, roll(q1[8], -1), roll(q1[0], -1))
    q0next = jnp.where(last, roll(q0[8], -1), roll(q0[0], -1))
    q0late = jnp.where(last, roll(q0[8], -2), roll(q0[1], -1))
    q0 = q0[:8] + [q0next, q0late]
    q1 = q1[:8] + [q1next]
    raw_slope = cut(jnp.where(raw > 0, 1.0, raw_decay))
    out = []
    for k in range(8):
        dact = q0[k + 2] + q1[k + 1] + q2[k]
        total = dact * raw_slope[k] + own[:, LANE * k : LANE * (k + 1)]
        out.append(total.astype(BF16).astype(F32))
    for b, block in enumerate(to_time(out)):
        grad[:, LANE * b : LANE * (b + 1)] = block.astype(BF16)


def segment(rel):
    me = lax.axis_index("clip") * lax.axis_size("tm") + lax.axis_index("tm")
    return me ^ rel


FETCH = ((4, 3, 1, 2), (7, None, 5, 6))


def cot_kernel(per_clip, own, *refs):
    pieces, (out, rows) = refs[:2], refs[2:]
    count, width = rows.shape
    chan = lax.axis_index("chan")

    def put(rel, piece):
        start = pl.multiple_of(segment(rel) * LANE, LANE)
        rows[pl.ds(start, LANE), :] = piece[...].astype(F32)

    put(0, own)
    for c in range(4):
        for n in range(2):
            for place in range(4):
                rel = FETCH[n][place]
                if rel is not None:
                    pl.when((chan ^ c) == place)(lambda: put(rel, pieces[c % 2].at[c // 2 * 2 + n]))
    value = rows[...]
    out[:, :width] = value.astype(BF16)
    at = lax.broadcasted_iota(jnp.int32, value.shape, 0)
    moved = jnp.where(at % per_clip == per_clip - 1, 0.0, pltpu.roll(value, count - 1, 0))
    out[:, width:] = moved.astype(BF16)


def gathered(order, pieces, left):
    ch = left.shape[0] // 4
    for p in range(len(order)):
        for k in range(4):
            left[ch * k : ch * (k + 1), LANE * p : LANE * (p + 1)] = pieces[
                ch * p : ch * (p + 1), LANE * k : LANE * (k + 1)
            ]
    return left[...]


def arranged(order, cots, right):
    for p, rel in enumerate(order):
        start = pl.multiple_of(segment(rel) * LANE, LANE)
        right[LANE * p : LANE * (p + 1), :] = cots[pl.ds(start, LANE), :]
    return right[...]


def part_kernel(order, pieces, cots, out, left, right):
    out[...] = dot(gathered(order, pieces, left), arranged(order, cots, right))


def down_kernel(
    orders, factor, one, two, cots, one_part, two_part, mine, out, first, second, left, right
):
    ch = out.shape[2]
    width = out.shape[3]
    step = pl.program_id(0)
    for i, (far, part) in enumerate(((one, one_part), (two, two_part))):

        @pl.when(step == i)
        def _():
            total = dot(gathered(orders[i], far, left), arranged(orders[i], cots, right))
            total = (total + part[...]) * factor
            for k in range(4):
                out[0, k] = total[ch * k : ch * (k + 1), width:]
                out[1, k] = total[ch * k : ch * (k + 1), :width]

    @pl.when(step == 0)
    def _():
        weight = (mine[...].astype(F32) + one[4 * ch :, :].astype(F32)) * factor
        for k in range(KRES):
            first[k] = weight[:, LANE * k : LANE * (k + 1)]
        second[...] = weight[:, LANE * KRES :]


VMEM = pl.BlockSpec(memory_space=pltpu.VMEM)
LIMIT = pltpu.CompilerParams(vmem_limit_bytes=20 << 20)


def near(value):
    return pltpu.with_memory_space_constraint(value, pltpu.VMEM)


def far(value):
    return pltpu.with_memory_space_constraint(value, pltpu.HBM)


def cost(micros):
    return pl.CostEstimate(flops=0, transcendentals=0, bytes_accessed=int(micros * 3.6e6))


def whole(value):
    return pl.BlockSpec(value.shape, lambda i: (0,) * value.ndim)


def call(kernel, name, micros, out_shape, *args, loads=0, scratch=(), alias=None):
    specs = [whole(v) if i < loads else VMEM for i, v in enumerate(args)]
    args = [far(v) if i < loads else near(v) for i, v in enumerate(args)]
    return pl.pallas_call(
        kernel,
        grid=(1,),
        in_specs=specs,
        out_specs=jax.tree.map(lambda _: VMEM, out_shape),
        out_shape=jax.tree.map(lambda s: pltpu.VMEM(s.shape, s.dtype), out_shape),
        scratch_shapes=scratch,
        input_output_aliases=alias or {},
        compiler_params=LIMIT,
        cost_estimate=cost(micros),
        name=name,
    )(*args)


def struct(shape, dtype=BF16):
    return jax.ShapeDtypeStruct(shape, dtype)


def down_call(orders, factor, *args):
    ch = args[-1].shape[0]
    rows, width = args[2].shape
    width //= 2
    kernel = lambda *refs: down_kernel(orders, factor, *refs)
    return pl.pallas_call(
        kernel,
        grid=(2,),
        in_specs=[VMEM] * len(args),
        out_specs=(
            pl.BlockSpec((2, 4, ch, width), lambda i: (0, i, 0, 0)),
            pl.BlockSpec((KRES, ch, LANE), lambda i: (0, 0, 0)),
            pl.BlockSpec((ch, LANE), lambda i: (0, 0)),
        ),
        out_shape=(
            struct((2, 8, ch, width), F32),
            struct((KRES, ch, LANE), F32),
            struct((ch, LANE), F32),
        ),
        scratch_shapes=[
            pltpu.VMEM((4 * ch, rows // 2), BF16),
            pltpu.VMEM((rows // 2, 2 * width), BF16),
        ],
        compiler_params=LIMIT,
        cost_estimate=cost(2),
        name="down",
    )(*[near(v) for v in args])


def along_chan(value, other):
    pairs = [(i, i ^ other) for i in range(lax.axis_size("chan"))]
    return lax.ppermute(value, "chan", pairs)


def along_group(value, other):
    count = lax.axis_size("clip") * lax.axis_size("tm")
    return lax.ppermute(value, ("clip", "tm"), [(i, i ^ other) for i in range(count)])


def swapped(value, first):
    low = range(first, lax.axis_size("tm") - 1, 2)
    pairs = [p for i in low for p in ((i, i + 1), (i + 1, i))]
    return lax.ppermute(value, "tm", pairs)


def fetch(value, n):
    places = lax.axis_size("chan")
    pairs = []
    for me in range(lax.axis_size("clip") * lax.axis_size("tm")):
        for place in range(places):
            rel = FETCH[n][place]
            if rel is not None:
                pairs.append(((me ^ rel) * places + place, me * places + place))
    return lax.ppermute(value, ("clip", "tm", "chan"), pairs)


def after(value, *others):
    return lax.optimization_barrier((value, *others))[0]


def on_device(signal, conv_first, conv_second, conv_down, cotangent):
    sig = signal[0].T
    second = conv_second.T
    cot = cotangent[0]
    ch, length = sig.shape
    count, width = cot.shape
    clips, times = lax.axis_size("clip"), lax.axis_size("tm")
    group = clips * times
    pack, edge = call(
        pack_kernel,
        "pack",
        3,
        (
            struct((ch, 2 * length + LANE * (KRES + 1))),
            struct((2 * ch, LANE)),
        ),
        sig,
        conv_first,
        second,
        cot,
        conv_down,
        loads=5,
    )
    pack_y = along_chan(pack, 2)
    even = swapped(edge, 0)
    odd = swapped(edge, 1)
    halo = call(merge_kernel, "merge", 0.1, struct((ch, LANE)), even, odd)
    halo_y = along_chan(halo, 2)
    small = (clips, times) == (2, 4)
    fetched = ()
    if small:
        source = after(cot, edge)
        fetched = fetch(source, 0), fetch(source, 1)
    pack_y = after(pack_y, halo_y, *fetched)
    pair = call(
        join_kernel,
        "join",
        0.1,
        struct((2 * ch, 2 * length + LANE * (KRES + 2))),
        pack,
        halo,
        pack_y,
        halo_y,
    )
    other = along_chan(pair, 1)
    one, two, hidden = call(
        forward_kernel,
        "forward",
        1,
        (
            struct((ch, length // 2)),
            struct((ch, length // 2)),
            struct((LANE, length + LANE), F32),
        ),
        pair,
        other,
    )
    grad, weight = call(
        backward_kernel,
        "backward",
        2,
        (struct((ch, length)), struct((ch, LANE * (KRES + 1)))),
        pair,
        other,
        hidden,
    )
    factor = float(1.0 / np.sqrt(np.float32(clips * times * (length // STRIDE))))
    if small:
        mine = after(jnp.stack(fetched), one)
        mine = jnp.concatenate([mine, along_chan(mine, 2)])
        cots = call(
            lambda *refs: cot_kernel(times * count, *refs),
            "cots",
            1,
            struct((group * count, 2 * width)),
            cot,
            mine,
            along_chan(mine, 1),
            scratch=[pltpu.VMEM((group * count, width), F32)],
        )
        two = jnp.concatenate([two, along_group(two, 2)])
        for step in (4, 2):
            both = along_group(jnp.concatenate([one, weight]), step)
            one = jnp.concatenate([one, both[: one.shape[0]]])
            weight = weight.astype(F32) + both[-ch:].astype(F32)
            weight = weight.astype(BF16)
        two = jnp.concatenate([two, along_group(two, 1)])
        one_far = along_group(jnp.concatenate([one, weight]), 1)
        two_far = along_group(two, 4)
        parts = [
            call(
                lambda *refs: part_kernel(order, *refs),
                name,
                1,
                struct((4 * ch, 2 * width), F32),
                half,
                cots,
                scratch=[
                    pltpu.VMEM((4 * ch, 4 * count), BF16),
                    pltpu.VMEM((4 * count, 2 * width), BF16),
                ],
            )
            for order, half, name in (((0, 4, 2, 6), one, "part1"), ((0, 2, 1, 3), two, "part2"))
        ]
        down, first, second = down_call(
            ((1, 5, 3, 7), (4, 6, 5, 7)), factor, one_far, two_far, cots, *parts, weight
        )
    else:
        feed = jnp.concatenate([one, two], axis=1)
        blocks = feed.reshape(ch, STRIDE, count).transpose(1, 0, 2).reshape(STRIDE * ch, count)
        rest = lax.ppermute(cot[:1], "tm", [(i + 1, i) for i in range(times - 1)])
        behind = dot(blocks, cot)
        front = dot(blocks, jnp.concatenate([cot[1:], rest]))
        down = jnp.stack([front, behind]) * factor
        down, weight = lax.psum((down, weight.astype(F32)), ("clip", "tm"))
        weight = weight * factor
        first = jnp.stack([weight[:, LANE * k : LANE * (k + 1)] for k in range(KRES)])
        second = weight[:, LANE * KRES :]
    return (
        grad.T[None],
        first,
        second.T,
        down.reshape(conv_down.shape),
    )


def solution(mesh):
    return jax.shard_map(
        on_device,
        mesh=mesh,
        in_specs=(
            P("clip", "tm", "chan"),
            P(None, "chan", None),
            P(None, "chan"),
            P(None, "chan", None),
            P("clip", "tm", None),
        ),
        out_specs=(
            P("clip", "tm", "chan"),
            P(None, "chan", None),
            P(None, "chan"),
            P(None, "chan", None),
        ),
        check_vma=False,
    )
```

time: 74.2 us -> 55.4 us (0.75)
  Pallas kernels: 22 us -> 8.36 us
  waiting for transfers between devices: 13.3 us -> 23.3 us
  local copies, waits for them, and re-layouts: 8.13 us -> 0.74 us
  starting transfers between devices: 26.9 us -> 21.8 us
  other arithmetic: 2.49 us -> 0.14 us
    pallas_call x7 -> x9, Pallas kernels: 22 us -> 8.36 us  [the longest x8 6.38 us: call(): pl.pallas_call(kernel, grid=(1,), in_specs=specs, out_specs=jax.tree.map(...]
    ppermute x12 -> x6, starting transfers between devices: 16.9 us -> 8.23 us  [along_group(): lax.ppermute(value, ('clip', 'tm'), [(i, i ^ other) for i in range(count)])]
    unnamed x43 -> x6, local copies, waits for them, and re-layouts: 6.84 us -> 0.69 us
    ppermute x12 -> x5, waiting for transfers between devices: 3.26 us -> 7.55 us  [along_chan(): return lax.ppermute(value, 'chan', pairs)]
    ppermute x2 -> x4, starting transfers between devices: 4.76 us -> 8.99 us  [the longest x2 7.03 us: fetch(): return lax.ppermute(value, ('clip', 'tm', 'chan'), pairs)]
    ppermute x12 -> x6, waiting for transfers between devices: 9.99 us -> 13.1 us  [along_group(): lax.ppermute(value, ('clip', 'tm'), [(i, i ^ other) for i in range(count)])]
    ppermute x2 -> x4, waiting for transfers between devices: 0.01 us -> 2.67 us  [the longest x2 2.67 us: swapped(): return lax.ppermute(value, 'tm', pairs)]
    concatenate x5 -> x4, other arithmetic: 1.58 us -> 0.07 us  [the longest x2 0.03 us: on_device(): both = along_group(jnp.concatenate([one, weight]), step)]
  transfers between devices with their start and end apart: 26 -> 15, of which waited for: 7 -> 9; matrix products, arithmetic and copies ran while one was open for 6% -> 2% of each run, Pallas kernels for 22% -> 6%
where the time goes in v2:
time: 55.4 us; the launch traced here: 55.2 us
  waiting for transfers between devices  23.3 us (42%)
  starting transfers between devices  21.8 us (39%)
  Pallas kernels  8.36 us (15%)
  between operations  0.85 us (2%)
  local copies, waits for them, and re-layouts  0.74 us (1%)
    ppermute x6, waiting for transfers between devices, along_group(): lax.ppermute(value, ('clip', 'tm'), [(i, i ^ other) for i in range(count)])  13.1 us
    ppermute x6, starting transfers between devices, along_group(): lax.ppermute(value, ('clip', 'tm'), [(i, i ^ other) for i in range(count)])  8.23 us
    ppermute x5, waiting for transfers between devices, along_chan(): return lax.ppermute(value, 'chan', pairs)  7.55 us
    ppermute x2, starting transfers between devices, fetch(): return lax.ppermute(value, ('clip', 'tm', 'chan'), pairs)  7.03 us
    pallas_call x8, Pallas kernels, call(): pl.pallas_call(kernel, grid=(1,), in_specs=specs, out_specs=jax.tree.map(...  6.38 us
    ppermute x5, starting transfers between devices, along_chan(): return lax.ppermute(value, 'chan', pairs)  4.53 us
    ppermute x2, waiting for transfers between devices, swapped(): return lax.ppermute(value, 'tm', pairs)  2.67 us
    pallas_call x1, Pallas kernels, down_call(): pl.pallas_call(kernel, grid=(2,), in_specs=[VMEM] * len(args), out_specs=...  1.98 us
  transfers between devices with their start and end apart: 15, of which 9 were waited for; matrix products, arithmetic and copies ran while one was open for 2% of the time, Pallas kernels for 6%

profile of v2, /device:TPU:0, one launch (start us, length us, event | category | flops | bytes accessed | tf_op | source)
XLA Modules:
  0.0 55.2 jit_solution(10218448541414970437)
XLA Ops:
  0.6 2.2 %pack.1 = (bf16[64,2560]{1,0:T(8,128)(2,1)S(1)}, bf16[128,128]{1,0:T(8,128)(2,1)S(1)}) custom-call(bf16[64,1024]{1,0:T(8,128)(2,1)} %bitcast.19, bf16[3,64,128]{2,1,0:T(8,128)(2,1)} %first.1, bf16[64,128]{1,0:T(8,128)(2,1)} %bitcast.20, bf16[128,512]{1,0:T(8,128)(2,1)} %bitcast.13, bf16[16,64,512]{2,1,0:T(8,128)(2,1)} %down.2), custom_call_target="tpu_custom_call" | custom-call | bytes 10800000 | tf_op jit(solution)/shard_map/pack/pallas_call | solution.py:316
  2.8 3.0 %collective-permute-start.2 = (bf16[64,2560]{1,0:T(8,128)(2,1)S(1)}, bf16[64,2560]{1,0:T(8,128)(2,1)S(1)}, u32[]{:S(2)}, u32[]{:S(2)}) collective-permute-start(bf16[64,2560]{1,0:T(8,128)(2,1)S(1)} %get-tuple-element.17.pack), channel_id=1, source_target_pairs={{0,2},{1,3},{2,0},{3,1},{4,6},{5,7},{6,4},{7,5},{8,10},{9,11},{10,... | collective-permute-start | bytes 983048 | tf_op jit(solution)/shard_map/ppermute | solution.py:365
  5.9 6.4 %collective-permute-start.5 = (bf16[128,512]{1,0:T(8,128)(2,1)}, bf16[128,512]{1,0:T(8,128)(2,1)S(1)}, u32[]{:S(2)}, u32[]{:S(2)}) collective-permute-start(bf16[128,512]{1,0:T(8,128)(2,1)} %bitcast.14), channel_id=1, source_target_pairs={{28,0},{22,2},{27,3},{24,4},{18,6},{31,7},{20,8},{30,10},{19,11},{... | collective-permute-start | bytes 393224 | tf_op jit(solution)/shard_map/ppermute | solution.py:387
  12.3 0.6 %collective-permute-start.4 = (bf16[128,512]{1,0:T(8,128)(2,1)}, bf16[128,512]{1,0:T(8,128)(2,1)S(1)}, u32[]{:S(2)}, u32[]{:S(2)}) collective-permute-start(bf16[128,512]{1,0:T(8,128)(2,1)} %bitcast.15), channel_id=1, source_target_pairs={{16,0},{13,1},{6,2},{11,3},{20,4},{9,5},{2,6},{15,7},{24,8},{5,9},... | collective-permute-start | bytes 393224 | tf_op jit(solution)/shard_map/ppermute | solution.py:387
  12.9 0.7 %collective-permute-start.1 = (bf16[128,128]{1,0:T(8,128)(2,1)S(1)}, bf16[128,128]{1,0:T(8,128)(2,1)S(1)}, u32[]{:S(2)}, u32[]{:S(2)}) collective-permute-start(bf16[128,128]{1,0:T(8,128)(2,1)S(1)} %get-tuple-element.18), channel_id=1, source_target_pairs={{4,8},{8,4},{5,9},{9,5},{6,10},{10,6},{7,11},{11,7},{20,24},{24,20... | collective-permute-start | bytes 98312 | tf_op jit(solution)/shard_map/ppermute | solution.py:376
  13.6 1.3 %collective-permute-start = (bf16[128,128]{1,0:T(8,128)(2,1)S(1)}, bf16[128,128]{1,0:T(8,128)(2,1)S(1)}, u32[]{:S(2)}, u32[]{:S(2)}) collective-permute-start(bf16[128,128]{1,0:T(8,128)(2,1)S(1)} %get-tuple-element.18), channel_id=1, source_target_pairs={{0,4},{4,0},{8,12},{12,8},{1,5},{5,1},{9,13},{13,9},{2,6},{6,2},{1... | collective-permute-start | bytes 98312 | tf_op jit(solution)/shard_map/ppermute | solution.py:376
  14.9 2.7 %collective-permute-done.even = bf16[128,128]{1,0:T(8,128)(2,1)S(1)} collective-permute-done((bf16[128,128]{1,0:T(8,128)(2,1)S(1)}, bf16[128,128]{1,0:T(8,128)(2,1)S(1)}, u32[]{:S(2)}, u32[]{:S(2)}) %collective-permute-start) | collective-permute-done | bytes 32800 | tf_op jit(solution)/shard_map/ppermute | solution.py:376
  17.6 1.3 %collective-permute-start.3 = (bf16[64,128]{1,0:T(8,128)(2,1)S(1)}, bf16[64,128]{1,0:T(8,128)(2,1)S(1)}, u32[]{:S(2)}, u32[]{:S(2)}) collective-permute-start(bf16[64,128]{1,0:T(8,128)(2,1)S(1)} %merge.1.halo), channel_id=1, source_target_pairs={{0,2},{1,3},{2,0},{3,1},{4,6},{5,7},{6,4},{7,5},{8,10},{9,11},{10,... | collective-permute-start | bytes 49160 | tf_op jit(solution)/shard_map/ppermute | solution.py:365
  18.8 2.5 %collective-permute-done.3.halo_y = bf16[64,128]{1,0:T(8,128)(2,1)S(1)} collective-permute-done((bf16[64,128]{1,0:T(8,128)(2,1)S(1)}, bf16[64,128]{1,0:T(8,128)(2,1)S(1)}, u32[]{:S(2)}, u32[]{:S(2)}) %collective-permute-start.3) | collective-permute-done | bytes 16416 | tf_op jit(solution)/shard_map/ppermute | solution.py:365
  21.4 0.1 collective-permute-start.6
  21.5 2.1 %collective-permute-done.6.other = bf16[128,2688]{1,0:T(8,128)(2,1)S(1)} collective-permute-done((bf16[128,2688]{1,0:T(8,128)(2,1)S(1)}, bf16[128,2688]{1,0:T(8,128)(2,1)S(1)}, u32[]{:S(2)}, u32[]{:S(2)}) %collective-permute-start.6) | collective-permute-done | bytes 688160 | tf_op jit(solution)/shard_map/ppermute | solution.py:365
  23.6 0.9 %forward.1 = (bf16[64,512]{1,0:T(8,128)(2,1)S(1)}, bf16[64,512]{1,0:T(8,128)(2,1)S(1)}, f32[128,1152]{1,0:T(8,128)S(1)}) custom-call(bf16[128,2688]{1,0:T(8,128)(2,1)S(1)} %join.1.pair, bf16[128,2688]{1,0:T(8,128)(2,1)S(1)} %collective-permute-done.6.other), custom_call_target="tpu_custom_call" | custom-call | bytes 3600000 | tf_op jit(solution)/shard_map/forward/pallas_call | solution.py:316
  24.5 2.3 %collective-permute-start.10 = (bf16[64,512]{1,0:T(8,128)(2,1)S(1)}, bf16[64,512]{1,0:T(8,128)(2,1)S(1)}, u32[]{:S(2)}, u32[]{:S(2)}) collective-permute-start(bf16[64,512]{1,0:T(8,128)(2,1)S(1)} %get-tuple-element.25), channel_id=1, source_target_pairs={{0,8},{4,12},{8,0},{12,4},{16,24},{20,28},{24,16},{28,20},{1,9},{5... | collective-permute-start | bytes 196616 | tf_op jit(solution)/shard_map/ppermute | solution.py:370
  26.8 1.7 %backward.1 = (bf16[64,1024]{1,0:T(8,128)(2,1)S(1)}, bf16[64,512]{1,0:T(8,128)(2,1)S(1)}) custom-call(bf16[128,2688]{1,0:T(8,128)(2,1)S(1)} %join.1.pair, bf16[128,2688]{1,0:T(8,128)(2,1)S(1)} %collective-permute-done.6.other, f32[128,1152]{1,0:T(8,128)S(1)} %get-tuple-element.21.hidden), custom_call_target="tpu_custom_call" | custom-call | bytes 7200000 | tf_op jit(solution)/shard_map/backward/pallas_call | solution.py:316
  28.5 1.6 %collective-permute-start.7 = (bf16[128,512]{1,0:T(8,128)(2,1)S(1)}, bf16[128,512]{1,0:T(8,128)(2,1)S(1)}, u32[]{:S(2)}, u32[]{:S(2)}) collective-permute-start(bf16[128,512]{1,0:T(8,128)(2,1)S(1)} %pad_maximum_fusion.4), channel_id=1, source_target_pairs={{0,16},{4,20},{8,24},{12,28},{16,0},{20,4},{24,8},{28,12},{1,17},{... | collective-permute-start | bytes 393224 | tf_op jit(solution)/shard_map/ppermute | solution.py:370
  30.1 0.1 collective-permute-start.13
  30.2 0.8 %collective-permute-done.10 = bf16[64,512]{1,0:T(8,128)(2,1)S(1)} collective-permute-done((bf16[64,512]{1,0:T(8,128)(2,1)S(1)}, bf16[64,512]{1,0:T(8,128)(2,1)S(1)}, u32[]{:S(2)}, u32[]{:S(2)}) %collective-permute-start.10) | collective-permute-done | bytes 65568 | tf_op jit(solution)/shard_map/ppermute | solution.py:370
  31.0 1.7 %collective-permute-start.11 = (bf16[128,512]{1,0:T(8,128)(2,1)S(1)}, bf16[128,512]{1,0:T(8,128)(2,1)S(1)}, u32[]{:S(2)}, u32[]{:S(2)}) collective-permute-start(bf16[128,512]{1,0:T(8,128)(2,1)S(1)} %pad_maximum_fusion.5), channel_id=1, source_target_pairs={{0,4},{4,0},{8,12},{12,8},{16,20},{20,16},{24,28},{28,24},{1,5},{5... | collective-permute-start | bytes 393224 | tf_op jit(solution)/shard_map/ppermute | solution.py:370
  32.7 1.1 %collective-permute-done.7 = bf16[128,512]{1,0:T(8,128)(2,1)S(1)} collective-permute-done((bf16[128,512]{1,0:T(8,128)(2,1)S(1)}, bf16[128,512]{1,0:T(8,128)(2,1)S(1)}, u32[]{:S(2)}, u32[]{:S(2)}) %collective-permute-start.7) | collective-permute-done | bytes 131104 | tf_op jit(solution)/shard_map/ppermute | solution.py:370
  33.9 1.0 %collective-permute-start.8 = (bf16[192,512]{1,0:T(8,128)(2,1)S(1)}, bf16[192,512]{1,0:T(8,128)(2,1)S(1)}, u32[]{:S(2)}, u32[]{:S(2)}) collective-permute-start(bf16[192,512]{1,0:T(8,128)(2,1)S(1)} %pad_maximum_fusion.3), channel_id=1, source_target_pairs={{0,8},{4,12},{8,0},{12,4},{16,24},{20,28},{24,16},{28,20},{1,9},{5... | collective-permute-start | bytes 589832 | tf_op jit(solution)/shard_map/ppermute | solution.py:370
  35.0 2.9 %collective-permute-done.13 = bf16[2,128,512]{2,1,0:T(8,128)(2,1)S(1)} collective-permute-done((bf16[2,128,512]{2,1,0:T(8,128)(2,1)S(1)}, bf16[2,128,512]{2,1,0:T(8,128)(2,1)S(1)}, u32[]{:S(2)}, u32[]{:S(2)}) %collective-permute-start.13) | collective-permute-done | bytes 262176 | tf_op jit(solution)/shard_map/ppermute | solution.py:365
  37.9 0.1 collective-permute-start.14
  38.0 6.9 %collective-permute-done.8 = bf16[192,512]{1,0:T(8,128)(2,1)S(1)} collective-permute-done((bf16[192,512]{1,0:T(8,128)(2,1)S(1)}, bf16[192,512]{1,0:T(8,128)(2,1)S(1)}, u32[]{:S(2)}, u32[]{:S(2)}) %collective-permute-start.8) | collective-permute-done | bytes 196640 | tf_op jit(solution)/shard_map/ppermute | solution.py:370
  45.0 0.1 collective-permute-start.9
  45.1 1.5 %collective-permute-start.12 = (bf16[256,512]{1,0:T(8,128)(2,1)S(1)}, bf16[256,512]{1,0:T(8,128)(2,1)S(1)}, u32[]{:S(2)}, u32[]{:S(2)}) collective-permute-start(bf16[256,512]{1,0:T(8,128)(2,1)S(1)} %constant_dynamic-update-slice_fusion.refs_0_), channel_id=1, source_target_pairs={{0,16},{4,20},{8,24},{12,28},{16,0},{20,4},{24,8},{28,12},{1,17},{... | collective-permute-start | bytes 786440 | tf_op jit(solution)/shard_map/ppermute | solution.py:370
  46.6 0.7 %copy.12 = bf16[1,1024,64]{1,2,0:T(8,128)(2,1)} copy(bf16[1,1024,64]{1,2,0:T(8,128)(2,1)S(1)} %bitcast.12) | data formatting | bytes 262144
  47.3 0.7 %cots.1.refs_1_.refs_2_ = bf16[1024,1024]{1,0:T(8,128)(2,1)S(1)} custom-call(bf16[128,512]{1,0:T(8,128)(2,1)S(1)} %bitcast.16, bf16[4,128,512]{2,1,0:T(8,128)(2,1)S(1)} %constant_dynamic-update-slice_fusion.3.refs_1_, bf16[4,128,512]{2,1,0:T(8,128)(2,1)S(1)} %collective-permute-done.14.refs_2_), custom_call_target="tpu_custom_call" | custom-call | bytes 3600000 | tf_op jit(solution)/shard_map/cots/pallas_call | solution.py:316
  48.0 0.5 part2.1.refs_4_
  48.5 0.4 part1.1.refs_3_
  48.9 4.1 %collective-permute-done.12.refs_1_ = bf16[256,512]{1,0:T(8,128)(2,1)S(1)} collective-permute-done((bf16[256,512]{1,0:T(8,128)(2,1)S(1)}, bf16[256,512]{1,0:T(8,128)(2,1)S(1)}, u32[]{:S(2)}, u32[]{:S(2)}) %collective-permute-start.12) | collective-permute-done | bytes 262176 | tf_op jit(solution)/shard_map/ppermute | solution.py:370
  53.1 0.1 collective-permute-done.9.refs_0_
  53.2 2.0 %down.3 = (f32[2,8,64,512]{3,2,1,0:T(8,128)}, f32[3,64,128]{2,1,0:T(8,128)}, f32[64,128]{1,0:T(8,128)}) custom-call(bf16[320,512]{1,0:T(8,128)(2,1)S(1)} %collective-permute-done.9.refs_0_, bf16[256,512]{1,0:T(8,128)(2,1)S(1)} %collective-permute-done.12.refs_1_, bf16[1024,1024]{1,0:T(8,128)(2,1)S(1)} %cots.1.refs_1_.refs_2_, f32[256,1024]{1,0:T(8,128)S(1)} %part1.1.refs_3_, ...), custom_call_target="tpu_custom_call" | custom-call | bytes 7200000 | tf_op jit(solution)/shard_map/down/pallas_call | solution.py:339
  (25 shorter events, 0.3 us)
Async XLA Ops:
  2.8 18.5 %collective-permute-start.2 = (bf16[64,2560]{1,0:T(8,128)(2,1)S(1)}, bf16[64,2560]{1,0:T(8,128)(2,1)S(1)}, u32[]{:S(2)}, u32[]{:S(2)}) collective-permute-start(bf16[64,2560]{1,0:T(8,128)(2,1)S(1)} %get-tuple-element.17.pack), channel_id=1, source_target_pairs={{0,2},{1,3},{2,0},{3,1},{4,6},{5,7},{6,4},{7,5},{8,10},{9,11},{10,... | collective-permute-start | bytes 983048 | tf_op jit(solution)/shard_map/ppermute | solution.py:365
  5.9 15.5 %collective-permute-start.5 = (bf16[128,512]{1,0:T(8,128)(2,1)}, bf16[128,512]{1,0:T(8,128)(2,1)S(1)}, u32[]{:S(2)}, u32[]{:S(2)}) collective-permute-start(bf16[128,512]{1,0:T(8,128)(2,1)} %bitcast.14), channel_id=1, source_target_pairs={{28,0},{22,2},{27,3},{24,4},{18,6},{31,7},{20,8},{30,10},{19,11},{... | collective-permute-start | bytes 393224 | tf_op jit(solution)/shard_map/ppermute | solution.py:387
  12.3 9.1 %collective-permute-start.4 = (bf16[128,512]{1,0:T(8,128)(2,1)}, bf16[128,512]{1,0:T(8,128)(2,1)S(1)}, u32[]{:S(2)}, u32[]{:S(2)}) collective-permute-start(bf16[128,512]{1,0:T(8,128)(2,1)} %bitcast.15), channel_id=1, source_target_pairs={{16,0},{13,1},{6,2},{11,3},{20,4},{9,5},{2,6},{15,7},{24,8},{5,9},... | collective-permute-start | bytes 393224 | tf_op jit(solution)/shard_map/ppermute | solution.py:387
  12.9 2.0 %collective-permute-start.1 = (bf16[128,128]{1,0:T(8,128)(2,1)S(1)}, bf16[128,128]{1,0:T(8,128)(2,1)S(1)}, u32[]{:S(2)}, u32[]{:S(2)}) collective-permute-start(bf16[128,128]{1,0:T(8,128)(2,1)S(1)} %get-tuple-element.18), channel_id=1, source_target_pairs={{4,8},{8,4},{5,9},{9,5},{6,10},{10,6},{7,11},{11,7},{20,24},{24,20... | collective-permute-start | bytes 98312 | tf_op jit(solution)/shard_map/ppermute | solution.py:376
  13.6 4.0 %collective-permute-start = (bf16[128,128]{1,0:T(8,128)(2,1)S(1)}, bf16[128,128]{1,0:T(8,128)(2,1)S(1)}, u32[]{:S(2)}, u32[]{:S(2)}) collective-permute-start(bf16[128,128]{1,0:T(8,128)(2,1)S(1)} %get-tuple-element.18), channel_id=1, source_target_pairs={{0,4},{4,0},{8,12},{12,8},{1,5},{5,1},{9,13},{13,9},{2,6},{6,2},{1... | collective-permute-start | bytes 98312 | tf_op jit(solution)/shard_map/ppermute | solution.py:376
  17.6 3.8 %collective-permute-start.3 = (bf16[64,128]{1,0:T(8,128)(2,1)S(1)}, bf16[64,128]{1,0:T(8,128)(2,1)S(1)}, u32[]{:S(2)}, u32[]{:S(2)}) collective-permute-start(bf16[64,128]{1,0:T(8,128)(2,1)S(1)} %merge.1.halo), channel_id=1, source_target_pairs={{0,2},{1,3},{2,0},{3,1},{4,6},{5,7},{6,4},{7,5},{8,10},{9,11},{10,... | collective-permute-start | bytes 49160 | tf_op jit(solution)/shard_map/ppermute | solution.py:365
  21.4 2.2 %collective-permute-start.6 = (bf16[128,2688]{1,0:T(8,128)(2,1)S(1)}, bf16[128,2688]{1,0:T(8,128)(2,1)S(1)}, u32[]{:S(2)}, u32[]{:S(2)}) collective-permute-start(bf16[128,2688]{1,0:T(8,128)(2,1)S(1)} %join.1.pair), channel_id=1, source_target_pairs={{0,1},{1,0},{2,3},{3,2},{4,5},{5,4},{6,7},{7,6},{8,9},{9,8},{10,11... | collective-permute-start | bytes 2064392 | tf_op jit(solution)/shard_map/ppermute | solution.py:365
  24.5 6.5 %collective-permute-start.10 = (bf16[64,512]{1,0:T(8,128)(2,1)S(1)}, bf16[64,512]{1,0:T(8,128)(2,1)S(1)}, u32[]{:S(2)}, u32[]{:S(2)}) collective-permute-start(bf16[64,512]{1,0:T(8,128)(2,1)S(1)} %get-tuple-element.25), channel_id=1, source_target_pairs={{0,8},{4,12},{8,0},{12,4},{16,24},{20,28},{24,16},{28,20},{1,9},{5... | collective-permute-start | bytes 196616 | tf_op jit(solution)/shard_map/ppermute | solution.py:370
  28.5 18.8 %copy-start = (bf16[1,128,512]{2,1,0:T(8,128)(2,1)S(1)}, bf16[1,128,512]{2,1,0:T(8,128)(2,1)}, u32[]{:S(2)}) copy-start(bf16[1,128,512]{2,1,0:T(8,128)(2,1)} %param.9) | copy-start | bytes 393220
  28.5 5.3 %collective-permute-start.7 = (bf16[128,512]{1,0:T(8,128)(2,1)S(1)}, bf16[128,512]{1,0:T(8,128)(2,1)S(1)}, u32[]{:S(2)}, u32[]{:S(2)}) collective-permute-start(bf16[128,512]{1,0:T(8,128)(2,1)S(1)} %pad_maximum_fusion.4), channel_id=1, source_target_pairs={{0,16},{4,20},{8,24},{12,28},{16,0},{20,4},{24,8},{28,12},{1,17},{... | collective-permute-start | bytes 393224 | tf_op jit(solution)/shard_map/ppermute | solution.py:370
  30.1 7.8 %collective-permute-start.13 = (bf16[2,128,512]{2,1,0:T(8,128)(2,1)S(1)}, bf16[2,128,512]{2,1,0:T(8,128)(2,1)S(1)}, u32[]{:S(2)}, u32[]{:S(2)}) collective-permute-start(bf16[2,128,512]{2,1,0:T(8,128)(2,1)S(1)} %pad_maximum_fusion.1), channel_id=1, source_target_pairs={{0,2},{1,3},{2,0},{3,1},{4,6},{5,7},{6,4},{7,5},{8,10},{9,11},{10,... | collective-permute-start | bytes 786440 | tf_op jit(solution)/shard_map/ppermute | solution.py:365
  31.0 14.0 %collective-permute-start.11 = (bf16[128,512]{1,0:T(8,128)(2,1)S(1)}, bf16[128,512]{1,0:T(8,128)(2,1)S(1)}, u32[]{:S(2)}, u32[]{:S(2)}) collective-permute-start(bf16[128,512]{1,0:T(8,128)(2,1)S(1)} %pad_maximum_fusion.5), channel_id=1, source_target_pairs={{0,4},{4,0},{8,12},{12,8},{16,20},{20,16},{24,28},{28,24},{1,5},{5... | collective-permute-start | bytes 393224 | tf_op jit(solution)/shard_map/ppermute | solution.py:370
  33.9 11.0 %collective-permute-start.8 = (bf16[192,512]{1,0:T(8,128)(2,1)S(1)}, bf16[192,512]{1,0:T(8,128)(2,1)S(1)}, u32[]{:S(2)}, u32[]{:S(2)}) collective-permute-start(bf16[192,512]{1,0:T(8,128)(2,1)S(1)} %pad_maximum_fusion.3), channel_id=1, source_target_pairs={{0,8},{4,12},{8,0},{12,4},{16,24},{20,28},{24,16},{28,20},{1,9},{5... | collective-permute-start | bytes 589832 | tf_op jit(solution)/shard_map/ppermute | solution.py:370
  37.9 9.4 %collective-permute-start.14 = (bf16[4,128,512]{2,1,0:T(8,128)(2,1)S(1)}, bf16[4,128,512]{2,1,0:T(8,128)(2,1)S(1)}, u32[]{:S(2)}, u32[]{:S(2)}) collective-permute-start(bf16[4,128,512]{2,1,0:T(8,128)(2,1)S(1)} %constant_dynamic-update-slice_fusion.3.refs_1_), channel_id=1, source_target_pairs={{0,1},{1,0},{2,3},{3,2},{4,5},{5,4},{6,7},{7,6},{8,9},{9,8},{10,11... | collective-permute-start | bytes 1572872 | tf_op jit(solution)/shard_map/ppermute | solution.py:365
  45.0 8.2 %collective-permute-start.9 = (bf16[320,512]{1,0:T(8,128)(2,1)S(1)}, bf16[320,512]{1,0:T(8,128)(2,1)S(1)}, u32[]{:S(2)}, u32[]{:S(2)}) collective-permute-start(bf16[320,512]{1,0:T(8,128)(2,1)S(1)} %pad_maximum_fusion), channel_id=1, source_target_pairs={{0,4},{4,0},{8,12},{12,8},{16,20},{20,16},{24,28},{28,24},{1,5},{5... | collective-permute-start | bytes 983048 | tf_op jit(solution)/shard_map/ppermute | solution.py:370
  45.1 8.0 %collective-permute-start.12 = (bf16[256,512]{1,0:T(8,128)(2,1)S(1)}, bf16[256,512]{1,0:T(8,128)(2,1)S(1)}, u32[]{:S(2)}, u32[]{:S(2)}) collective-permute-start(bf16[256,512]{1,0:T(8,128)(2,1)S(1)} %constant_dynamic-update-slice_fusion.refs_0_), channel_id=1, source_target_pairs={{0,16},{4,20},{8,24},{12,28},{16,0},{20,4},{24,8},{28,12},{1,17},{... | collective-permute-start | bytes 786440 | tf_op jit(solution)/shard_map/ppermute | solution.py:370

commit v3 on v2

--- a/solution.py
+++ b/solution.py
@@ -219,25 +219,22 @@
     return me ^ rel
 
 
-FETCH = ((4, 3, 1, 2), (7, None, 5, 6))
-
-
-def cot_kernel(per_clip, own, *refs):
-    pieces, (out, rows) = refs[:2], refs[2:]
+FETCH = (0, 3, 1, 2)
+
+
+def cot_kernel(per_clip, mine, others, out, rows):
     count, width = rows.shape
     chan = lax.axis_index("chan")
-
-    def put(rel, piece):
-        start = pl.multiple_of(segment(rel) * LANE, LANE)
-        rows[pl.ds(start, LANE), :] = piece[...].astype(F32)
-
-    put(0, own)
     for c in range(4):
-        for n in range(2):
+        for clip in range(2):
+            piece = (mine, others)[c % 2].at[clip * 2 + c // 2]
             for place in range(4):
-                rel = FETCH[n][place]
-                if rel is not None:
-                    pl.when((chan ^ c) == place)(lambda: put(rel, pieces[c % 2].at[c // 2 * 2 + n]))
+
+                @pl.when((chan ^ c) == place)
+                def _():
+                    start = pl.multiple_of(segment(FETCH[place] + 4 * clip) * LANE, LANE)
+                    rows[pl.ds(start, LANE), :] = piece[...].astype(F32)
+
     value = rows[...]
     out[:, :width] = value.astype(BF16)
     at = lax.broadcasted_iota(jnp.int32, value.shape, 0)
@@ -267,7 +264,7 @@
 
 
 def down_kernel(
-    orders, factor, one, two, cots, one_part, two_part, mine, out, first, second, left, right
+    orders, factor, one, two, cots, one_part, two_part, mine, other, out, first, second, left, right
 ):
     ch = out.shape[2]
     width = out.shape[3]
@@ -284,7 +281,7 @@
 
     @pl.when(step == 0)
     def _():
-        weight = (mine[...].astype(F32) + one[4 * ch :, :].astype(F32)) * factor
+        weight = (mine[...].astype(F32) + other[...].astype(F32)) * factor
         for k in range(KRES):
             first[k] = weight[:, LANE * k : LANE * (k + 1)]
         second[...] = weight[:, LANE * KRES :]
@@ -376,14 +373,12 @@
     return lax.ppermute(value, "tm", pairs)
 
 
-def fetch(value, n):
+def fetch(value):
     places = lax.axis_size("chan")
     pairs = []
     for me in range(lax.axis_size("clip") * lax.axis_size("tm")):
-        for place in range(places):
-            rel = FETCH[n][place]
-            if rel is not None:
-                pairs.append(((me ^ rel) * places + place, me * places + place))
+        for place, rel in enumerate(FETCH):
+            pairs.append(((me ^ rel) * places + place, me * places + place))
     return lax.ppermute(value, ("clip", "tm", "chan"), pairs)
 
 
@@ -423,7 +418,7 @@
     fetched = ()
     if small:
         source = after(cot, edge)
-        fetched = fetch(source, 0), fetch(source, 1)
+        fetched = (fetch(source),)
     pack_y = after(pack_y, halo_y, *fetched)
     pair = call(
         join_kernel,
@@ -459,27 +454,30 @@
     )
     factor = float(1.0 / np.sqrt(np.float32(clips * times * (length // STRIDE))))
     if small:
-        mine = after(jnp.stack(fetched), one)
-        mine = jnp.concatenate([mine, along_chan(mine, 2)])
+        two = two_x = jnp.concatenate([two, along_group(two, 2)])
+        both = along_group(jnp.concatenate([one, weight]), 4)
+        one = one_x = jnp.concatenate([one, both[:ch]])
+        weight = (weight.astype(F32) + both[ch:].astype(F32)).astype(BF16)
+        one = jnp.concatenate([one, along_group(one, 2)])
+        both = along_group(jnp.concatenate([two, weight]), 1)
+        two = jnp.concatenate([two, both[: 2 * ch]])
+        weight = (weight.astype(F32) + both[2 * ch :].astype(F32)).astype(BF16)
+        mine = after(fetched[0], two_x)
+        mine_y = along_chan(mine, 2)
+        cross = along_group(after(fetched[0], two_x), 4)
+        cross = jnp.concatenate([jnp.stack([mine, mine_y]), jnp.stack([cross, along_chan(cross, 2)])])
         cots = call(
             lambda *refs: cot_kernel(times * count, *refs),
             "cots",
             1,
             struct((group * count, 2 * width)),
-            cot,
-            mine,
-            along_chan(mine, 1),
+            cross,
+            along_chan(cross, 1),
             scratch=[pltpu.VMEM((group * count, width), F32)],
         )
-        two = jnp.concatenate([two, along_group(two, 2)])
-        for step in (4, 2):
-            both = along_group(jnp.concatenate([one, weight]), step)
-            one = jnp.concatenate([one, both[: one.shape[0]]])
-            weight = weight.astype(F32) + both[-ch:].astype(F32)
-            weight = weight.astype(BF16)
-        two = jnp.concatenate([two, along_group(two, 1)])
-        one_far = along_group(jnp.concatenate([one, weight]), 1)
+        one_far = along_group(one, 1)
         two_far = along_group(two, 4)
+        weights = (weight, along_group(weight, 2))
         parts = [
             call(
                 lambda *refs: part_kernel(order, *refs),
@@ -496,7 +494,7 @@
             for order, half, name in (((0, 4, 2, 6), one, "part1"), ((0, 2, 1, 3), two, "part2"))
         ]
         down, first, second = down_call(
-            ((1, 5, 3, 7), (4, 6, 5, 7)), factor, one_far, two_far, cots, *parts, weight
+            ((1, 5, 3, 7), (4, 6, 5, 7)), factor, one_far, two_far, cots, *parts, *weights
         )
     else:
         feed = jnp.concatenate([one, two], axis=1)

time: 55.4 us -> 51 us (0.921)
  waiting for transfers between devices: 23.3 us -> 18.1 us
  starting transfers between devices: 21.8 us -> 22.7 us
    ppermute x2 -> x1, starting transfers between devices: 7.03 us -> 1.55 us  [fetch(): return lax.ppermute(value, ('clip', 'tm', 'chan'), pairs)]
    ppermute x5 -> x6, waiting for transfers between devices: 7.55 us -> 2.3 us  [along_chan(): return lax.ppermute(value, 'chan', pairs)]
    ppermute x2, starting transfers between devices: 1.96 us -> 5.12 us  [swapped(): return lax.ppermute(value, 'tm', pairs)]
    ppermute x5 -> x6, starting transfers between devices: 4.53 us -> 7.49 us  [along_chan(): return lax.ppermute(value, 'chan', pairs)]
    ppermute x6 -> x8, waiting for transfers between devices: 13.1 us -> 13.6 us  [along_group(): lax.ppermute(value, ('clip', 'tm'), [(i, i ^ other) for i in range(count)])]
    ppermute x6 -> x8, starting transfers between devices: 8.23 us -> 8.55 us  [along_group(): lax.ppermute(value, ('clip', 'tm'), [(i, i ^ other) for i in range(count)])]
  transfers between devices with their start and end apart: 15 -> 17, of which waited for: 9 -> 9; matrix products, arithmetic and copies ran while one was open for 2% -> 2% of each run, Pallas kernels for 6% -> 8%
where the time goes in v3:
time: 51 us; the launch traced here: 50.8 us
  starting transfers between devices  22.7 us (45%)
  waiting for transfers between devices  18.1 us (35%)
  Pallas kernels  8.42 us (17%)
  between operations  0.8 us (2%)
  local copies, waits for them, and re-layouts  0.67 us (1%)
    ppermute x8, waiting for transfers between devices, along_group(): lax.ppermute(value, ('clip', 'tm'), [(i, i ^ other) for i in range(count)])  13.6 us
    ppermute x8, starting transfers between devices, along_group(): lax.ppermute(value, ('clip', 'tm'), [(i, i ^ other) for i in range(count)])  8.55 us
    ppermute x6, starting transfers between devices, along_chan(): return lax.ppermute(value, 'chan', pairs)  7.49 us
    pallas_call x8, Pallas kernels, call(): pl.pallas_call(kernel, grid=(1,), in_specs=specs, out_specs=jax.tree.map(...  6.43 us
    ppermute x2, starting transfers between devices, swapped(): return lax.ppermute(value, 'tm', pairs)  5.12 us
    ppermute x6, waiting for transfers between devices, along_chan(): return lax.ppermute(value, 'chan', pairs)  2.3 us
    ppermute x2, waiting for transfers between devices, swapped(): return lax.ppermute(value, 'tm', pairs)  2.14 us
    pallas_call x1, Pallas kernels, down_call(): pl.pallas_call(kernel, grid=(2,), in_specs=[VMEM] * len(args), out_specs=...  1.99 us
  transfers between devices with their start and end apart: 17, of which 9 were waited for; matrix products, arithmetic and copies ran while one was open for 2% of the time, Pallas kernels for 8%

profile of v3, /device:TPU:0, one launch (start us, length us, event | category | flops | bytes accessed | tf_op | source)
XLA Modules:
  0.0 50.8 jit_solution(9288194686404306357)
XLA Ops:
  0.6 2.2 %pack.1 = (bf16[64,2560]{1,0:T(8,128)(2,1)S(1)}, bf16[128,128]{1,0:T(8,128)(2,1)S(1)}) custom-call(bf16[64,1024]{1,0:T(8,128)(2,1)} %bitcast.15, bf16[3,64,128]{2,1,0:T(8,128)(2,1)} %first.1, bf16[64,128]{1,0:T(8,128)(2,1)} %bitcast.22, bf16[128,512]{1,0:T(8,128)(2,1)} %bitcast.16, bf16[16,64,512]{2,1,0:T(8,128)(2,1)} %down.2), custom_call_target="tpu_custom_call" | custom-call | bytes 10800000 | tf_op jit(solution)/shard_map/pack/pallas_call | solution.py:313
  2.8 3.0 %collective-permute-start.2 = (bf16[64,2560]{1,0:T(8,128)(2,1)S(1)}, bf16[64,2560]{1,0:T(8,128)(2,1)S(1)}, u32[]{:S(2)}, u32[]{:S(2)}) collective-permute-start(bf16[64,2560]{1,0:T(8,128)(2,1)S(1)} %get-tuple-element.16.pack), channel_id=1, source_target_pairs={{0,2},{1,3},{2,0},{3,1},{4,6},{5,7},{6,4},{7,5},{8,10},{9,11},{10,... | collective-permute-start | bytes 983048 | tf_op jit(solution)/shard_map/ppermute | solution.py:362
  5.9 1.6 %collective-permute-start.4 = (bf16[128,512]{1,0:T(8,128)(2,1)}, bf16[128,512]{1,0:T(8,128)(2,1)S(1)}, u32[]{:S(2)}, u32[]{:S(2)}) collective-permute-start(bf16[128,512]{1,0:T(8,128)(2,1)} %bitcast.17), channel_id=1, source_target_pairs={{0,0},{13,1},{6,2},{11,3},{4,4},{9,5},{2,6},{15,7},{8,8},{5,9},{14... | collective-permute-start | bytes 393224 | tf_op jit(solution)/shard_map/ppermute | solution.py:382
  7.4 0.7 %collective-permute-start.1 = (bf16[128,128]{1,0:T(8,128)(2,1)S(1)}, bf16[128,128]{1,0:T(8,128)(2,1)S(1)}, u32[]{:S(2)}, u32[]{:S(2)}) collective-permute-start(bf16[128,128]{1,0:T(8,128)(2,1)S(1)} %get-tuple-element.17), channel_id=1, source_target_pairs={{4,8},{8,4},{5,9},{9,5},{6,10},{10,6},{7,11},{11,7},{20,24},{24,20... | collective-permute-start | bytes 98312 | tf_op jit(solution)/shard_map/ppermute | solution.py:373
  8.1 4.5 %collective-permute-start = (bf16[128,128]{1,0:T(8,128)(2,1)S(1)}, bf16[128,128]{1,0:T(8,128)(2,1)S(1)}, u32[]{:S(2)}, u32[]{:S(2)}) collective-permute-start(bf16[128,128]{1,0:T(8,128)(2,1)S(1)} %get-tuple-element.17), channel_id=1, source_target_pairs={{0,4},{4,0},{8,12},{12,8},{1,5},{5,1},{9,13},{13,9},{2,6},{6,2},{1... | collective-permute-start | bytes 98312 | tf_op jit(solution)/shard_map/ppermute | solution.py:373
  12.5 2.1 %collective-permute-done.even = bf16[128,128]{1,0:T(8,128)(2,1)S(1)} collective-permute-done((bf16[128,128]{1,0:T(8,128)(2,1)S(1)}, bf16[128,128]{1,0:T(8,128)(2,1)S(1)}, u32[]{:S(2)}, u32[]{:S(2)}) %collective-permute-start) | collective-permute-done | bytes 32800 | tf_op jit(solution)/shard_map/ppermute | solution.py:373
  14.7 2.3 %collective-permute-start.3 = (bf16[64,128]{1,0:T(8,128)(2,1)S(1)}, bf16[64,128]{1,0:T(8,128)(2,1)S(1)}, u32[]{:S(2)}, u32[]{:S(2)}) collective-permute-start(bf16[64,128]{1,0:T(8,128)(2,1)S(1)} %merge.1.halo), channel_id=1, source_target_pairs={{0,2},{1,3},{2,0},{3,1},{4,6},{5,7},{6,4},{7,5},{8,10},{9,11},{10,... | collective-permute-start | bytes 49160 | tf_op jit(solution)/shard_map/ppermute | solution.py:362
  17.0 1.7 %collective-permute-done.3.halo_y = bf16[64,128]{1,0:T(8,128)(2,1)S(1)} collective-permute-done((bf16[64,128]{1,0:T(8,128)(2,1)S(1)}, bf16[64,128]{1,0:T(8,128)(2,1)S(1)}, u32[]{:S(2)}, u32[]{:S(2)}) %collective-permute-start.3) | collective-permute-done | bytes 16416 | tf_op jit(solution)/shard_map/ppermute | solution.py:362
  18.7 0.1 collective-permute-start.5
  18.8 1.6 %collective-permute-start.13 = (bf16[128,512]{1,0:T(8,128)(2,1)S(1)}, bf16[128,512]{1,0:T(8,128)(2,1)S(1)}, u32[]{:S(2)}, u32[]{:S(2)}) collective-permute-start(bf16[128,512]{1,0:T(8,128)(2,1)S(1)} %collective-permute-done.4), channel_id=1, source_target_pairs={{0,16},{4,20},{8,24},{12,28},{16,0},{20,4},{24,8},{28,12},{1,17},{... | collective-permute-start | bytes 393224 | tf_op jit(solution)/shard_map/ppermute | solution.py:367
  20.4 0.6 %collective-permute-done.5.other = bf16[128,2688]{1,0:T(8,128)(2,1)S(1)} collective-permute-done((bf16[128,2688]{1,0:T(8,128)(2,1)S(1)}, bf16[128,2688]{1,0:T(8,128)(2,1)S(1)}, u32[]{:S(2)}, u32[]{:S(2)}) %collective-permute-start.5) | collective-permute-done | bytes 688160 | tf_op jit(solution)/shard_map/ppermute | solution.py:362
  21.0 0.9 %forward.1 = (bf16[64,512]{1,0:T(8,128)(2,1)S(1)}, bf16[64,512]{1,0:T(8,128)(2,1)S(1)}, f32[128,1152]{1,0:T(8,128)S(1)}) custom-call(bf16[128,2688]{1,0:T(8,128)(2,1)S(1)} %join.1.pair, bf16[128,2688]{1,0:T(8,128)(2,1)S(1)} %collective-permute-done.5.other), custom_call_target="tpu_custom_call" | custom-call | bytes 3600000 | tf_op jit(solution)/shard_map/forward/pallas_call | solution.py:313
  21.8 1.7 %backward.1 = (bf16[64,1024]{1,0:T(8,128)(2,1)S(1)}, bf16[64,512]{1,0:T(8,128)(2,1)S(1)}) custom-call(bf16[128,2688]{1,0:T(8,128)(2,1)S(1)} %join.1.pair, bf16[128,2688]{1,0:T(8,128)(2,1)S(1)} %collective-permute-done.5.other, f32[128,1152]{1,0:T(8,128)S(1)} %get-tuple-element.20.hidden), custom_call_target="tpu_custom_call" | custom-call | bytes 7200000 | tf_op jit(solution)/shard_map/backward/pallas_call | solution.py:313
  23.5 1.6 %collective-permute-start.6 = (bf16[128,512]{1,0:T(8,128)(2,1)S(1)}, bf16[128,512]{1,0:T(8,128)(2,1)S(1)}, u32[]{:S(2)}, u32[]{:S(2)}) collective-permute-start(bf16[128,512]{1,0:T(8,128)(2,1)S(1)} %pad_maximum_fusion.5), channel_id=1, source_target_pairs={{0,16},{4,20},{8,24},{12,28},{16,0},{20,4},{24,8},{28,12},{1,17},{... | collective-permute-start | bytes 393224 | tf_op jit(solution)/shard_map/ppermute | solution.py:367
  25.1 2.0 %collective-permute-start.12 = (bf16[128,512]{1,0:T(8,128)(2,1)S(1)}, bf16[128,512]{1,0:T(8,128)(2,1)S(1)}, u32[]{:S(2)}, u32[]{:S(2)}) collective-permute-start(bf16[128,512]{1,0:T(8,128)(2,1)S(1)} %collective-permute-done.4), channel_id=1, source_target_pairs={{0,2},{1,3},{2,0},{3,1},{4,6},{5,7},{6,4},{7,5},{8,10},{9,11},{10,... | collective-permute-start | bytes 393224 | tf_op jit(solution)/shard_map/ppermute | solution.py:362
  27.1 1.8 %collective-permute-start.9 = (bf16[64,512]{1,0:T(8,128)(2,1)S(1)}, bf16[64,512]{1,0:T(8,128)(2,1)S(1)}, u32[]{:S(2)}, u32[]{:S(2)}) collective-permute-start(bf16[64,512]{1,0:T(8,128)(2,1)S(1)} %get-tuple-element.24), channel_id=1, source_target_pairs={{0,8},{4,12},{8,0},{12,4},{16,24},{20,28},{24,16},{28,20},{1,9},{5... | collective-permute-start | bytes 196616 | tf_op jit(solution)/shard_map/ppermute | solution.py:367
  28.9 0.2 collective-permute-done.6
  29.1 1.9 %collective-permute-start.7 = (bf16[128,512]{1,0:T(8,128)(2,1)S(1)}, bf16[128,512]{1,0:T(8,128)(2,1)S(1)}, u32[]{:S(2)}, u32[]{:S(2)}) collective-permute-start(bf16[128,512]{1,0:T(8,128)(2,1)S(1)} %pad_maximum_fusion.4), channel_id=1, source_target_pairs={{0,8},{4,12},{8,0},{12,4},{16,24},{20,28},{24,16},{28,20},{1,9},{5... | collective-permute-start | bytes 393224 | tf_op jit(solution)/shard_map/ppermute | solution.py:367
  31.0 5.0 %collective-permute-done.9 = bf16[64,512]{1,0:T(8,128)(2,1)S(1)} collective-permute-done((bf16[64,512]{1,0:T(8,128)(2,1)S(1)}, bf16[64,512]{1,0:T(8,128)(2,1)S(1)}, u32[]{:S(2)}, u32[]{:S(2)}) %collective-permute-start.9) | collective-permute-done | bytes 65568 | tf_op jit(solution)/shard_map/ppermute | solution.py:367
  36.1 0.1 collective-permute-start.10
  36.3 0.1 collective-permute-start.15
  36.3 3.0 %collective-permute-done.7 = bf16[128,512]{1,0:T(8,128)(2,1)S(1)} collective-permute-done((bf16[128,512]{1,0:T(8,128)(2,1)S(1)}, bf16[128,512]{1,0:T(8,128)(2,1)S(1)}, u32[]{:S(2)}, u32[]{:S(2)}) %collective-permute-start.7) | collective-permute-done | bytes 131104 | tf_op jit(solution)/shard_map/ppermute | solution.py:367
  39.4 2.6 %collective-permute-done.10 = bf16[192,512]{1,0:T(8,128)(2,1)S(1)} collective-permute-done((bf16[192,512]{1,0:T(8,128)(2,1)S(1)}, bf16[192,512]{1,0:T(8,128)(2,1)S(1)}, u32[]{:S(2)}, u32[]{:S(2)}) %collective-permute-start.10) | collective-permute-done | bytes 196640 | tf_op jit(solution)/shard_map/ppermute | solution.py:367
  42.1 0.5 collective-permute-start.11
  42.6 1.1 %collective-permute-start.16 = (bf16[64,512]{1,0:T(8,128)(2,1)S(1)}, bf16[64,512]{1,0:T(8,128)(2,1)S(1)}, u32[]{:S(2)}, u32[]{:S(2)}) collective-permute-start(bf16[64,512]{1,0:T(8,128)(2,1)S(1)} %add_convert_fusion.refs_5_), channel_id=1, source_target_pairs={{0,8},{4,12},{8,0},{12,4},{16,24},{20,28},{24,16},{28,20},{1,9},{5... | collective-permute-start | bytes 196616 | tf_op jit(solution)/shard_map/ppermute | solution.py:367
  43.7 0.8 %cots.1.refs_1_.refs_2_ = bf16[1024,1024]{1,0:T(8,128)(2,1)S(1)} custom-call(bf16[4,128,512]{2,1,0:T(8,128)(2,1)S(1)} %pad_maximum_fusion.refs_0_, bf16[4,128,512]{2,1,0:T(8,128)(2,1)S(1)} %collective-permute-done.15.refs_1_), custom_call_target="tpu_custom_call" | custom-call | bytes 3600000 | tf_op jit(solution)/shard_map/cots/pallas_call | solution.py:313
  44.5 0.7 %copy.9 = bf16[1,1024,64]{1,2,0:T(8,128)(2,1)} copy(bf16[1,1024,64]{1,2,0:T(8,128)(2,1)S(1)} %bitcast.14) | data formatting | bytes 262144
  45.1 0.4 part1.1.refs_3_
  45.6 0.5 part2.1.refs_4_
  46.0 1.9 %collective-permute-done.16.refs_6_ = bf16[64,512]{1,0:T(8,128)(2,1)S(1)} collective-permute-done((bf16[64,512]{1,0:T(8,128)(2,1)S(1)}, bf16[64,512]{1,0:T(8,128)(2,1)S(1)}, u32[]{:S(2)}, u32[]{:S(2)}) %collective-permute-start.16) | collective-permute-done | bytes 65568 | tf_op jit(solution)/shard_map/ppermute | solution.py:367
  47.9 0.9 %collective-permute-done.8.refs_0_ = bf16[256,512]{1,0:T(8,128)(2,1)S(1)} collective-permute-done((bf16[256,512]{1,0:T(8,128)(2,1)S(1)}, bf16[256,512]{1,0:T(8,128)(2,1)S(1)}, u32[]{:S(2)}, u32[]{:S(2)}) %collective-permute-start.8) | collective-permute-done | bytes 262176 | tf_op jit(solution)/shard_map/ppermute | solution.py:367
  48.9 2.0 %down.3 = (f32[2,8,64,512]{3,2,1,0:T(8,128)}, f32[3,64,128]{2,1,0:T(8,128)}, f32[64,128]{1,0:T(8,128)}) custom-call(bf16[256,512]{1,0:T(8,128)(2,1)S(1)} %collective-permute-done.8.refs_0_, bf16[256,512]{1,0:T(8,128)(2,1)S(1)} %collective-permute-done.11.refs_1_, bf16[1024,1024]{1,0:T(8,128)(2,1)S(1)} %cots.1.refs_1_.refs_2_, f32[256,1024]{1,0:T(8,128)S(1)} %part1.1.refs_3_, ...), custom_call_target="tpu_custom_call" | custom-call | bytes 7200000 | tf_op jit(solution)/shard_map/down/pallas_call | solution.py:336
  (22 shorter events, 0.4 us)
Async XLA Ops:
  2.8 15.9 %collective-permute-start.2 = (bf16[64,2560]{1,0:T(8,128)(2,1)S(1)}, bf16[64,2560]{1,0:T(8,128)(2,1)S(1)}, u32[]{:S(2)}, u32[]{:S(2)}) collective-permute-start(bf16[64,2560]{1,0:T(8,128)(2,1)S(1)} %get-tuple-element.16.pack), channel_id=1, source_target_pairs={{0,2},{1,3},{2,0},{3,1},{4,6},{5,7},{6,4},{7,5},{8,10},{9,11},{10,... | collective-permute-start | bytes 983048 | tf_op jit(solution)/shard_map/ppermute | solution.py:362
  5.9 12.8 %collective-permute-start.4 = (bf16[128,512]{1,0:T(8,128)(2,1)}, bf16[128,512]{1,0:T(8,128)(2,1)S(1)}, u32[]{:S(2)}, u32[]{:S(2)}) collective-permute-start(bf16[128,512]{1,0:T(8,128)(2,1)} %bitcast.17), channel_id=1, source_target_pairs={{0,0},{13,1},{6,2},{11,3},{4,4},{9,5},{2,6},{15,7},{8,8},{5,9},{14... | collective-permute-start | bytes 393224 | tf_op jit(solution)/shard_map/ppermute | solution.py:382
  7.4 5.1 %collective-permute-start.1 = (bf16[128,128]{1,0:T(8,128)(2,1)S(1)}, bf16[128,128]{1,0:T(8,128)(2,1)S(1)}, u32[]{:S(2)}, u32[]{:S(2)}) collective-permute-start(bf16[128,128]{1,0:T(8,128)(2,1)S(1)} %get-tuple-element.17), channel_id=1, source_target_pairs={{4,8},{8,4},{5,9},{9,5},{6,10},{10,6},{7,11},{11,7},{20,24},{24,20... | collective-permute-start | bytes 98312 | tf_op jit(solution)/shard_map/ppermute | solution.py:373
  8.1 6.6 %collective-permute-start = (bf16[128,128]{1,0:T(8,128)(2,1)S(1)}, bf16[128,128]{1,0:T(8,128)(2,1)S(1)}, u32[]{:S(2)}, u32[]{:S(2)}) collective-permute-start(bf16[128,128]{1,0:T(8,128)(2,1)S(1)} %get-tuple-element.17), channel_id=1, source_target_pairs={{0,4},{4,0},{8,12},{12,8},{1,5},{5,1},{9,13},{13,9},{2,6},{6,2},{1... | collective-permute-start | bytes 98312 | tf_op jit(solution)/shard_map/ppermute | solution.py:373
  14.7 4.0 %collective-permute-start.3 = (bf16[64,128]{1,0:T(8,128)(2,1)S(1)}, bf16[64,128]{1,0:T(8,128)(2,1)S(1)}, u32[]{:S(2)}, u32[]{:S(2)}) collective-permute-start(bf16[64,128]{1,0:T(8,128)(2,1)S(1)} %merge.1.halo), channel_id=1, source_target_pairs={{0,2},{1,3},{2,0},{3,1},{4,6},{5,7},{6,4},{7,5},{8,10},{9,11},{10,... | collective-permute-start | bytes 49160 | tf_op jit(solution)/shard_map/ppermute | solution.py:362
  18.7 2.2 %collective-permute-start.5 = (bf16[128,2688]{1,0:T(8,128)(2,1)S(1)}, bf16[128,2688]{1,0:T(8,128)(2,1)S(1)}, u32[]{:S(2)}, u32[]{:S(2)}) collective-permute-start(bf16[128,2688]{1,0:T(8,128)(2,1)S(1)} %join.1.pair), channel_id=1, source_target_pairs={{0,1},{1,0},{2,3},{3,2},{4,5},{5,4},{6,7},{7,6},{8,9},{9,8},{10,11... | collective-permute-start | bytes 2064392 | tf_op jit(solution)/shard_map/ppermute | solution.py:362
  18.8 8.3 %collective-permute-start.13 = (bf16[128,512]{1,0:T(8,128)(2,1)S(1)}, bf16[128,512]{1,0:T(8,128)(2,1)S(1)}, u32[]{:S(2)}, u32[]{:S(2)}) collective-permute-start(bf16[128,512]{1,0:T(8,128)(2,1)S(1)} %collective-permute-done.4), channel_id=1, source_target_pairs={{0,16},{4,20},{8,24},{12,28},{16,0},{20,4},{24,8},{28,12},{1,17},{... | collective-permute-start | bytes 393224 | tf_op jit(solution)/shard_map/ppermute | solution.py:367
  23.5 5.6 %collective-permute-start.6 = (bf16[128,512]{1,0:T(8,128)(2,1)S(1)}, bf16[128,512]{1,0:T(8,128)(2,1)S(1)}, u32[]{:S(2)}, u32[]{:S(2)}) collective-permute-start(bf16[128,512]{1,0:T(8,128)(2,1)S(1)} %pad_maximum_fusion.5), channel_id=1, source_target_pairs={{0,16},{4,20},{8,24},{12,28},{16,0},{20,4},{24,8},{28,12},{1,17},{... | collective-permute-start | bytes 393224 | tf_op jit(solution)/shard_map/ppermute | solution.py:367
  25.1 11.1 %collective-permute-start.12 = (bf16[128,512]{1,0:T(8,128)(2,1)S(1)}, bf16[128,512]{1,0:T(8,128)(2,1)S(1)}, u32[]{:S(2)}, u32[]{:S(2)}) collective-permute-start(bf16[128,512]{1,0:T(8,128)(2,1)S(1)} %collective-permute-done.4), channel_id=1, source_target_pairs={{0,2},{1,3},{2,0},{3,1},{4,6},{5,7},{6,4},{7,5},{8,10},{9,11},{10,... | collective-permute-start | bytes 393224 | tf_op jit(solution)/shard_map/ppermute | solution.py:362
  27.1 9.1 %collective-permute-start.14 = (bf16[128,512]{1,0:T(8,128)(2,1)S(1)}, bf16[128,512]{1,0:T(8,128)(2,1)S(1)}, u32[]{:S(2)}, u32[]{:S(2)}) collective-permute-start(bf16[128,512]{1,0:T(8,128)(2,1)S(1)} %collective-permute-done.13), channel_id=1, source_target_pairs={{0,2},{1,3},{2,0},{3,1},{4,6},{5,7},{6,4},{7,5},{8,10},{9,11},{10,... | collective-permute-start | bytes 393224 | tf_op jit(solution)/shard_map/ppermute | solution.py:362
  27.1 9.0 %collective-permute-start.9 = (bf16[64,512]{1,0:T(8,128)(2,1)S(1)}, bf16[64,512]{1,0:T(8,128)(2,1)S(1)}, u32[]{:S(2)}, u32[]{:S(2)}) collective-permute-start(bf16[64,512]{1,0:T(8,128)(2,1)S(1)} %get-tuple-element.24), channel_id=1, source_target_pairs={{0,8},{4,12},{8,0},{12,4},{16,24},{20,28},{24,16},{28,20},{1,9},{5... | collective-permute-start | bytes 196616 | tf_op jit(solution)/shard_map/ppermute | solution.py:367
  29.1 10.2 %collective-permute-start.7 = (bf16[128,512]{1,0:T(8,128)(2,1)S(1)}, bf16[128,512]{1,0:T(8,128)(2,1)S(1)}, u32[]{:S(2)}, u32[]{:S(2)}) collective-permute-start(bf16[128,512]{1,0:T(8,128)(2,1)S(1)} %pad_maximum_fusion.4), channel_id=1, source_target_pairs={{0,8},{4,12},{8,0},{12,4},{16,24},{20,28},{24,16},{28,20},{1,9},{5... | collective-permute-start | bytes 393224 | tf_op jit(solution)/shard_map/ppermute | solution.py:367
  36.1 5.9 %collective-permute-start.10 = (bf16[192,512]{1,0:T(8,128)(2,1)S(1)}, bf16[192,512]{1,0:T(8,128)(2,1)S(1)}, u32[]{:S(2)}, u32[]{:S(2)}) collective-permute-start(bf16[192,512]{1,0:T(8,128)(2,1)S(1)} %pad_maximum_fusion.3), channel_id=1, source_target_pairs={{0,4},{4,0},{8,12},{12,8},{16,20},{20,16},{24,28},{28,24},{1,5},{5... | collective-permute-start | bytes 589832 | tf_op jit(solution)/shard_map/ppermute | solution.py:367
  36.3 7.4 %collective-permute-start.15 = (bf16[4,128,512]{2,1,0:T(8,128)(2,1)S(1)}, bf16[4,128,512]{2,1,0:T(8,128)(2,1)S(1)}, u32[]{:S(2)}, u32[]{:S(2)}) collective-permute-start(bf16[4,128,512]{2,1,0:T(8,128)(2,1)S(1)} %pad_maximum_fusion.refs_0_), channel_id=1, source_target_pairs={{0,1},{1,0},{2,3},{3,2},{4,5},{5,4},{6,7},{7,6},{8,9},{9,8},{10,11... | collective-permute-start | bytes 1572872 | tf_op jit(solution)/shard_map/ppermute | solution.py:362
  39.3 9.5 %collective-permute-start.8 = (bf16[256,512]{1,0:T(8,128)(2,1)S(1)}, bf16[256,512]{1,0:T(8,128)(2,1)S(1)}, u32[]{:S(2)}, u32[]{:S(2)}) collective-permute-start(bf16[256,512]{1,0:T(8,128)(2,1)S(1)} %pad_maximum_fusion.1.refs_0_), channel_id=1, source_target_pairs={{0,4},{4,0},{8,12},{12,8},{16,20},{20,16},{24,28},{28,24},{1,5},{5... | collective-permute-start | bytes 786440 | tf_op jit(solution)/shard_map/ppermute | solution.py:367
  42.1 6.8 %collective-permute-start.11 = (bf16[256,512]{1,0:T(8,128)(2,1)S(1)}, bf16[256,512]{1,0:T(8,128)(2,1)S(1)}, u32[]{:S(2)}, u32[]{:S(2)}) collective-permute-start(bf16[256,512]{1,0:T(8,128)(2,1)S(1)} %pad_maximum_fusion.2.refs_0_), channel_id=1, source_target_pairs={{0,16},{4,20},{8,24},{12,28},{16,0},{20,4},{24,8},{28,12},{1,17},{... | collective-permute-start | bytes 786440 | tf_op jit(solution)/shard_map/ppermute | solution.py:367
  42.6 5.3 %collective-permute-start.16 = (bf16[64,512]{1,0:T(8,128)(2,1)S(1)}, bf16[64,512]{1,0:T(8,128)(2,1)S(1)}, u32[]{:S(2)}, u32[]{:S(2)}) collective-permute-start(bf16[64,512]{1,0:T(8,128)(2,1)S(1)} %add_convert_fusion.refs_5_), channel_id=1, source_target_pairs={{0,8},{4,12},{8,0},{12,4},{16,24},{20,28},{24,16},{28,20},{1,9},{5... | collective-permute-start | bytes 196616 | tf_op jit(solution)/shard_map/ppermute | solution.py:367

commit v4 on v3

--- a/solution.py
+++ b/solution.py
@@ -259,21 +259,22 @@
     return right[...]
 
 
-def part_kernel(order, pieces, cots, out, left, right):
+def part_kernel(order, later, pieces, cots, out, rows, left, right):
     out[...] = dot(gathered(order, pieces, left), arranged(order, cots, right))
+    arranged(later, cots, rows)
 
 
 def down_kernel(
-    orders, factor, one, two, cots, one_part, two_part, mine, other, out, first, second, left, right
+    orders, factor, one, two, one_part, one_rows, two_part, two_rows, mine, other, out, first, second, left
 ):
     ch = out.shape[2]
     width = out.shape[3]
     step = pl.program_id(0)
-    for i, (far, part) in enumerate(((one, one_part), (two, two_part))):
+    for i, (far, part, rows) in enumerate(((one, one_part, one_rows), (two, two_part, two_rows))):
 
         @pl.when(step == i)
         def _():
-            total = dot(gathered(orders[i], far, left), arranged(orders[i], cots, right))
+            total = dot(gathered(orders[i], far, left), rows[...])
             total = (total + part[...]) * factor
             for k in range(4):
                 out[0, k] = total[ch * k : ch * (k + 1), width:]
@@ -330,7 +331,7 @@
 
 def down_call(orders, factor, *args):
     ch = args[-1].shape[0]
-    rows, width = args[2].shape
+    rows, width = args[3].shape
     width //= 2
     kernel = lambda *refs: down_kernel(orders, factor, *refs)
     return pl.pallas_call(
@@ -348,8 +349,7 @@
             struct((ch, LANE), F32),
         ),
         scratch_shapes=[
-            pltpu.VMEM((4 * ch, rows // 2), BF16),
-            pltpu.VMEM((rows // 2, 2 * width), BF16),
+            pltpu.VMEM((4 * ch, rows), BF16),
         ],
         compiler_params=LIMIT,
         cost_estimate=cost(2),
@@ -478,12 +478,15 @@
         one_far = along_group(one, 1)
         two_far = along_group(two, 4)
         weights = (weight, along_group(weight, 2))
-        parts = [
-            call(
-                lambda *refs: part_kernel(order, *refs),
+        near_orders = ((0, 4, 2, 6), (0, 2, 1, 3))
+        far_orders = ((1, 5, 3, 7), (4, 6, 5, 7))
+        parts = []
+        for order, later, half, name in zip(near_orders, far_orders, (one, two), ("part1", "part2")):
+            parts += call(
+                lambda *refs: part_kernel(order, later, *refs),
                 name,
                 1,
-                struct((4 * ch, 2 * width), F32),
+                (struct((4 * ch, 2 * width), F32), struct((4 * count, 2 * width))),
                 half,
                 cots,
                 scratch=[
@@ -491,11 +494,7 @@
                     pltpu.VMEM((4 * count, 2 * width), BF16),
                 ],
             )
-            for order, half, name in (((0, 4, 2, 6), one, "part1"), ((0, 2, 1, 3), two, "part2"))
-        ]
-        down, first, second = down_call(
-            ((1, 5, 3, 7), (4, 6, 5, 7)), factor, one_far, two_far, cots, *parts, *weights
-        )
+        down, first, second = down_call(far_orders, factor, one_far, two_far, *parts, *weights)
     else:
         feed = jnp.concatenate([one, two], axis=1)
         blocks = feed.reshape(ch, STRIDE, count).transpose(1, 0, 2).reshape(STRIDE * ch, count)

time: 51 us -> 50.3 us (0.986)
  waiting for transfers between devices: 18.1 us -> 13.4 us
  starting transfers between devices: 22.7 us -> 26.5 us
    ppermute x8, starting transfers between devices: 8.55 us -> 13.8 us  [along_group(): lax.ppermute(value, ('clip', 'tm'), [(i, i ^ other) for i in range(count)])]
    ppermute x8, waiting for transfers between devices: 13.6 us -> 9.59 us  [along_group(): lax.ppermute(value, ('clip', 'tm'), [(i, i ^ other) for i in range(count)])]
    ppermute x2, starting transfers between devices: 5.12 us -> 2.23 us  [swapped(): return lax.ppermute(value, 'tm', pairs)]
    ppermute x6, starting transfers between devices: 7.49 us -> 8.91 us  [along_chan(): return lax.ppermute(value, 'chan', pairs)]
  transfers between devices with their start and end apart: 17 -> 17, of which waited for: 9 -> 8; matrix products, arithmetic and copies ran while one was open for 2% -> 2% of each run, Pallas kernels for 8% -> 9%
where the time goes in v4:
time: 50.3 us; the launch traced here: 50.1 us
  starting transfers between devices  26.5 us (53%)
  waiting for transfers between devices  13.4 us (27%)
  Pallas kernels  8.52 us (17%)
  between operations  0.79 us (2%)
  local copies, waits for them, and re-layouts  0.67 us (1%)
    ppermute x8, starting transfers between devices, along_group(): lax.ppermute(value, ('clip', 'tm'), [(i, i ^ other) for i in range(count)])  13.8 us
    ppermute x8, waiting for transfers between devices, along_group(): lax.ppermute(value, ('clip', 'tm'), [(i, i ^ other) for i in range(count)])  9.59 us
    ppermute x6, starting transfers between devices, along_chan(): return lax.ppermute(value, 'chan', pairs)  8.91 us
    pallas_call x8, Pallas kernels, call(): pl.pallas_call(kernel, grid=(1,), in_specs=specs, out_specs=jax.tree.map(...  6.57 us
    ppermute x2, starting transfers between devices, swapped(): return lax.ppermute(value, 'tm', pairs)  2.23 us
    ppermute x6, waiting for transfers between devices, along_chan(): return lax.ppermute(value, 'chan', pairs)  2.15 us
    pallas_call x1, Pallas kernels, down_call(): pl.pallas_call(kernel, grid=(2,), in_specs=[VMEM] * len(args), out_specs=...  1.94 us
    ppermute x2, waiting for transfers between devices, swapped(): return lax.ppermute(value, 'tm', pairs)  1.68 us
  transfers between devices with their start and end apart: 17, of which 8 were waited for; matrix products, arithmetic and copies ran while one was open for 2% of the time, Pallas kernels for 9%

profile of v4, /device:TPU:0, one launch (start us, length us, event | category | flops | bytes accessed | tf_op | source)
XLA Modules:
  0.0 50.1 jit_solution(1321101310026679693)
XLA Ops:
  0.6 2.2 %pack.1 = (bf16[64,2560]{1,0:T(8,128)(2,1)S(1)}, bf16[128,128]{1,0:T(8,128)(2,1)S(1)}) custom-call(bf16[64,1024]{1,0:T(8,128)(2,1)} %bitcast.15, bf16[3,64,128]{2,1,0:T(8,128)(2,1)} %first.1, bf16[64,128]{1,0:T(8,128)(2,1)} %bitcast.22, bf16[128,512]{1,0:T(8,128)(2,1)} %bitcast.16, bf16[16,64,512]{2,1,0:T(8,128)(2,1)} %down.2), custom_call_target="tpu_custom_call" | custom-call | bytes 10800000 | tf_op jit(solution)/shard_map/pack/pallas_call | solution.py:314
  2.8 3.0 %collective-permute-start.2 = (bf16[64,2560]{1,0:T(8,128)(2,1)S(1)}, bf16[64,2560]{1,0:T(8,128)(2,1)S(1)}, u32[]{:S(2)}, u32[]{:S(2)}) collective-permute-start(bf16[64,2560]{1,0:T(8,128)(2,1)S(1)} %get-tuple-element.20.pack), channel_id=1, source_target_pairs={{0,2},{1,3},{2,0},{3,1},{4,6},{5,7},{6,4},{7,5},{8,10},{9,11},{10,... | collective-permute-start | bytes 983048 | tf_op jit(solution)/shard_map/ppermute | solution.py:362
  5.9 1.6 %collective-permute-start.4 = (bf16[128,512]{1,0:T(8,128)(2,1)}, bf16[128,512]{1,0:T(8,128)(2,1)S(1)}, u32[]{:S(2)}, u32[]{:S(2)}) collective-permute-start(bf16[128,512]{1,0:T(8,128)(2,1)} %bitcast.17), channel_id=1, source_target_pairs={{0,0},{13,1},{6,2},{11,3},{4,4},{9,5},{2,6},{15,7},{8,8},{5,9},{14... | collective-permute-start | bytes 393224 | tf_op jit(solution)/shard_map/ppermute | solution.py:382
  7.4 1.6 %collective-permute-start = (bf16[128,128]{1,0:T(8,128)(2,1)S(1)}, bf16[128,128]{1,0:T(8,128)(2,1)S(1)}, u32[]{:S(2)}, u32[]{:S(2)}) collective-permute-start(bf16[128,128]{1,0:T(8,128)(2,1)S(1)} %get-tuple-element.21), channel_id=1, source_target_pairs={{0,4},{4,0},{8,12},{12,8},{1,5},{5,1},{9,13},{13,9},{2,6},{6,2},{1... | collective-permute-start | bytes 98312 | tf_op jit(solution)/shard_map/ppermute | solution.py:373
  9.0 0.7 %collective-permute-start.1 = (bf16[128,128]{1,0:T(8,128)(2,1)S(1)}, bf16[128,128]{1,0:T(8,128)(2,1)S(1)}, u32[]{:S(2)}, u32[]{:S(2)}) collective-permute-start(bf16[128,128]{1,0:T(8,128)(2,1)S(1)} %get-tuple-element.21), channel_id=1, source_target_pairs={{4,8},{8,4},{5,9},{9,5},{6,10},{10,6},{7,11},{11,7},{20,24},{24,20... | collective-permute-start | bytes 98312 | tf_op jit(solution)/shard_map/ppermute | solution.py:373
  9.7 1.7 %collective-permute-done.even = bf16[128,128]{1,0:T(8,128)(2,1)S(1)} collective-permute-done((bf16[128,128]{1,0:T(8,128)(2,1)S(1)}, bf16[128,128]{1,0:T(8,128)(2,1)S(1)}, u32[]{:S(2)}, u32[]{:S(2)}) %collective-permute-start) | collective-permute-done | bytes 32800 | tf_op jit(solution)/shard_map/ppermute | solution.py:373
  11.4 3.7 %collective-permute-start.3 = (bf16[64,128]{1,0:T(8,128)(2,1)S(1)}, bf16[64,128]{1,0:T(8,128)(2,1)S(1)}, u32[]{:S(2)}, u32[]{:S(2)}) collective-permute-start(bf16[64,128]{1,0:T(8,128)(2,1)S(1)} %merge.1.halo), channel_id=1, source_target_pairs={{0,2},{1,3},{2,0},{3,1},{4,6},{5,7},{6,4},{7,5},{8,10},{9,11},{10,... | collective-permute-start | bytes 49160 | tf_op jit(solution)/shard_map/ppermute | solution.py:362
  15.1 1.7 %collective-permute-done.3.halo_y = bf16[64,128]{1,0:T(8,128)(2,1)S(1)} collective-permute-done((bf16[64,128]{1,0:T(8,128)(2,1)S(1)}, bf16[64,128]{1,0:T(8,128)(2,1)S(1)}, u32[]{:S(2)}, u32[]{:S(2)}) %collective-permute-start.3) | collective-permute-done | bytes 16416 | tf_op jit(solution)/shard_map/ppermute | solution.py:362
  16.9 1.7 %collective-permute-start.13 = (bf16[128,512]{1,0:T(8,128)(2,1)S(1)}, bf16[128,512]{1,0:T(8,128)(2,1)S(1)}, u32[]{:S(2)}, u32[]{:S(2)}) collective-permute-start(bf16[128,512]{1,0:T(8,128)(2,1)S(1)} %collective-permute-done.4), channel_id=1, source_target_pairs={{0,16},{4,20},{8,24},{12,28},{16,0},{20,4},{24,8},{28,12},{1,17},{... | collective-permute-start | bytes 393224 | tf_op jit(solution)/shard_map/ppermute | solution.py:367
  18.6 0.4 collective-permute-done.5.other
  19.1 0.9 %forward.1 = (bf16[64,512]{1,0:T(8,128)(2,1)S(1)}, bf16[64,512]{1,0:T(8,128)(2,1)S(1)}, f32[128,1152]{1,0:T(8,128)S(1)}) custom-call(bf16[128,2688]{1,0:T(8,128)(2,1)S(1)} %join.1.pair, bf16[128,2688]{1,0:T(8,128)(2,1)S(1)} %collective-permute-done.5.other), custom_call_target="tpu_custom_call" | custom-call | bytes 3600000 | tf_op jit(solution)/shard_map/forward/pallas_call | solution.py:314
  19.9 1.7 %backward.1 = (bf16[64,1024]{1,0:T(8,128)(2,1)S(1)}, bf16[64,512]{1,0:T(8,128)(2,1)S(1)}) custom-call(bf16[128,2688]{1,0:T(8,128)(2,1)S(1)} %join.1.pair, bf16[128,2688]{1,0:T(8,128)(2,1)S(1)} %collective-permute-done.5.other, f32[128,1152]{1,0:T(8,128)S(1)} %get-tuple-element.24.hidden), custom_call_target="tpu_custom_call" | custom-call | bytes 7200000 | tf_op jit(solution)/shard_map/backward/pallas_call | solution.py:314
  21.6 1.7 %collective-permute-start.6 = (bf16[128,512]{1,0:T(8,128)(2,1)S(1)}, bf16[128,512]{1,0:T(8,128)(2,1)S(1)}, u32[]{:S(2)}, u32[]{:S(2)}) collective-permute-start(bf16[128,512]{1,0:T(8,128)(2,1)S(1)} %pad_maximum_fusion.5), channel_id=1, source_target_pairs={{0,16},{4,20},{8,24},{12,28},{16,0},{20,4},{24,8},{28,12},{1,17},{... | collective-permute-start | bytes 393224 | tf_op jit(solution)/shard_map/ppermute | solution.py:367
  23.3 1.9 %collective-permute-start.12 = (bf16[128,512]{1,0:T(8,128)(2,1)S(1)}, bf16[128,512]{1,0:T(8,128)(2,1)S(1)}, u32[]{:S(2)}, u32[]{:S(2)}) collective-permute-start(bf16[128,512]{1,0:T(8,128)(2,1)S(1)} %collective-permute-done.4), channel_id=1, source_target_pairs={{0,2},{1,3},{2,0},{3,1},{4,6},{5,7},{6,4},{7,5},{8,10},{9,11},{10,... | collective-permute-start | bytes 393224 | tf_op jit(solution)/shard_map/ppermute | solution.py:362
  25.2 0.1 collective-permute-start.14
  25.4 4.2 %collective-permute-start.9 = (bf16[64,512]{1,0:T(8,128)(2,1)S(1)}, bf16[64,512]{1,0:T(8,128)(2,1)S(1)}, u32[]{:S(2)}, u32[]{:S(2)}) collective-permute-start(bf16[64,512]{1,0:T(8,128)(2,1)S(1)} %get-tuple-element.28), channel_id=1, source_target_pairs={{0,8},{4,12},{8,0},{12,4},{16,24},{20,28},{24,16},{28,20},{1,9},{5... | collective-permute-start | bytes 196616 | tf_op jit(solution)/shard_map/ppermute | solution.py:367
  29.6 2.1 %collective-permute-start.7 = (bf16[128,512]{1,0:T(8,128)(2,1)S(1)}, bf16[128,512]{1,0:T(8,128)(2,1)S(1)}, u32[]{:S(2)}, u32[]{:S(2)}) collective-permute-start(bf16[128,512]{1,0:T(8,128)(2,1)S(1)} %pad_maximum_fusion.4), channel_id=1, source_target_pairs={{0,8},{4,12},{8,0},{12,4},{16,24},{20,28},{24,16},{28,20},{1,9},{5... | collective-permute-start | bytes 393224 | tf_op jit(solution)/shard_map/ppermute | solution.py:367
  31.7 0.1 collective-permute-done.9
  31.9 2.0 %collective-permute-start.10 = (bf16[192,512]{1,0:T(8,128)(2,1)S(1)}, bf16[192,512]{1,0:T(8,128)(2,1)S(1)}, u32[]{:S(2)}, u32[]{:S(2)}) collective-permute-start(bf16[192,512]{1,0:T(8,128)(2,1)S(1)} %pad_maximum_fusion.3), channel_id=1, source_target_pairs={{0,4},{4,0},{8,12},{12,8},{16,20},{20,16},{24,28},{28,24},{1,5},{5... | collective-permute-start | bytes 589832 | tf_op jit(solution)/shard_map/ppermute | solution.py:367
  33.9 0.1 collective-permute-start.15
  34.0 4.5 %collective-permute-done.7 = bf16[128,512]{1,0:T(8,128)(2,1)S(1)} collective-permute-done((bf16[128,512]{1,0:T(8,128)(2,1)S(1)}, bf16[128,512]{1,0:T(8,128)(2,1)S(1)}, u32[]{:S(2)}, u32[]{:S(2)}) %collective-permute-start.7) | collective-permute-done | bytes 131104 | tf_op jit(solution)/shard_map/ppermute | solution.py:367
  38.5 0.1 collective-permute-start.8
  38.6 1.8 %collective-permute-done.10 = bf16[192,512]{1,0:T(8,128)(2,1)S(1)} collective-permute-done((bf16[192,512]{1,0:T(8,128)(2,1)S(1)}, bf16[192,512]{1,0:T(8,128)(2,1)S(1)}, u32[]{:S(2)}, u32[]{:S(2)}) %collective-permute-start.10) | collective-permute-done | bytes 196640 | tf_op jit(solution)/shard_map/ppermute | solution.py:367
  40.4 1.4 %collective-permute-start.11 = (bf16[256,512]{1,0:T(8,128)(2,1)S(1)}, bf16[256,512]{1,0:T(8,128)(2,1)S(1)}, u32[]{:S(2)}, u32[]{:S(2)}) collective-permute-start(bf16[256,512]{1,0:T(8,128)(2,1)S(1)} %pad_maximum_fusion.2.refs_0_), channel_id=1, source_target_pairs={{0,16},{4,20},{8,24},{12,28},{16,0},{20,4},{24,8},{28,12},{1,17},{... | collective-permute-start | bytes 786440 | tf_op jit(solution)/shard_map/ppermute | solution.py:367
  41.8 0.7 %collective-permute-start.16 = (bf16[64,512]{1,0:T(8,128)(2,1)S(1)}, bf16[64,512]{1,0:T(8,128)(2,1)S(1)}, u32[]{:S(2)}, u32[]{:S(2)}) collective-permute-start(bf16[64,512]{1,0:T(8,128)(2,1)S(1)} %add_convert_fusion.refs_6_), channel_id=1, source_target_pairs={{0,8},{4,12},{8,0},{12,4},{16,24},{20,28},{24,16},{28,20},{1,9},{5... | collective-permute-start | bytes 196616 | tf_op jit(solution)/shard_map/ppermute | solution.py:367
  42.5 0.8 %cots.1.refs_1_ = bf16[1024,1024]{1,0:T(8,128)(2,1)S(1)} custom-call(bf16[4,128,512]{2,1,0:T(8,128)(2,1)S(1)} %pad_maximum_fusion.refs_0_, bf16[4,128,512]{2,1,0:T(8,128)(2,1)S(1)} %collective-permute-done.15.refs_1_), custom_call_target="tpu_custom_call" | custom-call | bytes 3600000 | tf_op jit(solution)/shard_map/cots/pallas_call | solution.py:314
  43.3 0.7 %copy.9 = bf16[1,1024,64]{1,2,0:T(8,128)(2,1)} copy(bf16[1,1024,64]{1,2,0:T(8,128)(2,1)S(1)} %bitcast.14) | data formatting | bytes 262144
  43.9 0.5 %part1.1 = (f32[256,1024]{1,0:T(8,128)S(1)}, bf16[512,1024]{1,0:T(8,128)(2,1)S(1)}) custom-call(bf16[256,512]{1,0:T(8,128)(2,1)S(1)} %pad_maximum_fusion.1.refs_0_, bf16[1024,1024]{1,0:T(8,128)(2,1)S(1)} %cots.1.refs_1_), custom_call_target="tpu_custom_call" | custom-call | bytes 3600000 | tf_op jit(solution)/shard_map/part1/pallas_call | solution.py:314
  44.4 0.5 %part2.1 = (f32[256,1024]{1,0:T(8,128)S(1)}, bf16[512,1024]{1,0:T(8,128)(2,1)S(1)}) custom-call(bf16[256,512]{1,0:T(8,128)(2,1)S(1)} %pad_maximum_fusion.2.refs_0_, bf16[1024,1024]{1,0:T(8,128)(2,1)S(1)} %cots.1.refs_1_), custom_call_target="tpu_custom_call" | custom-call | bytes 3600000 | tf_op jit(solution)/shard_map/part2/pallas_call | solution.py:314
  45.0 2.7 %collective-permute-done.16.refs_7_ = bf16[64,512]{1,0:T(8,128)(2,1)S(1)} collective-permute-done((bf16[64,512]{1,0:T(8,128)(2,1)S(1)}, bf16[64,512]{1,0:T(8,128)(2,1)S(1)}, u32[]{:S(2)}, u32[]{:S(2)}) %collective-permute-start.16) | collective-permute-done | bytes 65568 | tf_op jit(solution)/shard_map/ppermute | solution.py:367
  47.7 0.5 collective-permute-done.8.refs_0_
  48.1 1.9 %down.3 = (f32[2,8,64,512]{3,2,1,0:T(8,128)}, f32[3,64,128]{2,1,0:T(8,128)}, f32[64,128]{1,0:T(8,128)}) custom-call(bf16[256,512]{1,0:T(8,128)(2,1)S(1)} %collective-permute-done.8.refs_0_, bf16[256,512]{1,0:T(8,128)(2,1)S(1)} %collective-permute-done.11.refs_1_, f32[256,1024]{1,0:T(8,128)S(1)} %get-tuple-element.29.refs_2_, ...), custom_call_target="tpu_custom_call" | custom-call | bytes 7200000 | tf_op jit(solution)/shard_map/down/pallas_call | solution.py:337
  (22 shorter events, 0.4 us)
Async XLA Ops:
  2.8 14.0 %collective-permute-start.2 = (bf16[64,2560]{1,0:T(8,128)(2,1)S(1)}, bf16[64,2560]{1,0:T(8,128)(2,1)S(1)}, u32[]{:S(2)}, u32[]{:S(2)}) collective-permute-start(bf16[64,2560]{1,0:T(8,128)(2,1)S(1)} %get-tuple-element.20.pack), channel_id=1, source_target_pairs={{0,2},{1,3},{2,0},{3,1},{4,6},{5,7},{6,4},{7,5},{8,10},{9,11},{10,... | collective-permute-start | bytes 983048 | tf_op jit(solution)/shard_map/ppermute | solution.py:362
  5.9 10.9 %collective-permute-start.4 = (bf16[128,512]{1,0:T(8,128)(2,1)}, bf16[128,512]{1,0:T(8,128)(2,1)S(1)}, u32[]{:S(2)}, u32[]{:S(2)}) collective-permute-start(bf16[128,512]{1,0:T(8,128)(2,1)} %bitcast.17), channel_id=1, source_target_pairs={{0,0},{13,1},{6,2},{11,3},{4,4},{9,5},{2,6},{15,7},{8,8},{5,9},{14... | collective-permute-start | bytes 393224 | tf_op jit(solution)/shard_map/ppermute | solution.py:382
  7.4 3.9 %collective-permute-start = (bf16[128,128]{1,0:T(8,128)(2,1)S(1)}, bf16[128,128]{1,0:T(8,128)(2,1)S(1)}, u32[]{:S(2)}, u32[]{:S(2)}) collective-permute-start(bf16[128,128]{1,0:T(8,128)(2,1)S(1)} %get-tuple-element.21), channel_id=1, source_target_pairs={{0,4},{4,0},{8,12},{12,8},{1,5},{5,1},{9,13},{13,9},{2,6},{6,2},{1... | collective-permute-start | bytes 98312 | tf_op jit(solution)/shard_map/ppermute | solution.py:373
  9.0 2.3 %collective-permute-start.1 = (bf16[128,128]{1,0:T(8,128)(2,1)S(1)}, bf16[128,128]{1,0:T(8,128)(2,1)S(1)}, u32[]{:S(2)}, u32[]{:S(2)}) collective-permute-start(bf16[128,128]{1,0:T(8,128)(2,1)S(1)} %get-tuple-element.21), channel_id=1, source_target_pairs={{4,8},{8,4},{5,9},{9,5},{6,10},{10,6},{7,11},{11,7},{20,24},{24,20... | collective-permute-start | bytes 98312 | tf_op jit(solution)/shard_map/ppermute | solution.py:373
  11.4 5.4 %collective-permute-start.3 = (bf16[64,128]{1,0:T(8,128)(2,1)S(1)}, bf16[64,128]{1,0:T(8,128)(2,1)S(1)}, u32[]{:S(2)}, u32[]{:S(2)}) collective-permute-start(bf16[64,128]{1,0:T(8,128)(2,1)S(1)} %merge.1.halo), channel_id=1, source_target_pairs={{0,2},{1,3},{2,0},{3,1},{4,6},{5,7},{6,4},{7,5},{8,10},{9,11},{10,... | collective-permute-start | bytes 49160 | tf_op jit(solution)/shard_map/ppermute | solution.py:362
  16.9 2.2 %collective-permute-start.5 = (bf16[128,2688]{1,0:T(8,128)(2,1)S(1)}, bf16[128,2688]{1,0:T(8,128)(2,1)S(1)}, u32[]{:S(2)}, u32[]{:S(2)}) collective-permute-start(bf16[128,2688]{1,0:T(8,128)(2,1)S(1)} %join.1.pair), channel_id=1, source_target_pairs={{0,1},{1,0},{2,3},{3,2},{4,5},{5,4},{6,7},{7,6},{8,9},{9,8},{10,11... | collective-permute-start | bytes 2064392 | tf_op jit(solution)/shard_map/ppermute | solution.py:362
  16.9 8.3 %collective-permute-start.13 = (bf16[128,512]{1,0:T(8,128)(2,1)S(1)}, bf16[128,512]{1,0:T(8,128)(2,1)S(1)}, u32[]{:S(2)}, u32[]{:S(2)}) collective-permute-start(bf16[128,512]{1,0:T(8,128)(2,1)S(1)} %collective-permute-done.4), channel_id=1, source_target_pairs={{0,16},{4,20},{8,24},{12,28},{16,0},{20,4},{24,8},{28,12},{1,17},{... | collective-permute-start | bytes 393224 | tf_op jit(solution)/shard_map/ppermute | solution.py:367
  21.6 8.0 %collective-permute-start.6 = (bf16[128,512]{1,0:T(8,128)(2,1)S(1)}, bf16[128,512]{1,0:T(8,128)(2,1)S(1)}, u32[]{:S(2)}, u32[]{:S(2)}) collective-permute-start(bf16[128,512]{1,0:T(8,128)(2,1)S(1)} %pad_maximum_fusion.5), channel_id=1, source_target_pairs={{0,16},{4,20},{8,24},{12,28},{16,0},{20,4},{24,8},{28,12},{1,17},{... | collective-permute-start | bytes 393224 | tf_op jit(solution)/shard_map/ppermute | solution.py:367
  23.3 10.5 %collective-permute-start.12 = (bf16[128,512]{1,0:T(8,128)(2,1)S(1)}, bf16[128,512]{1,0:T(8,128)(2,1)S(1)}, u32[]{:S(2)}, u32[]{:S(2)}) collective-permute-start(bf16[128,512]{1,0:T(8,128)(2,1)S(1)} %collective-permute-done.4), channel_id=1, source_target_pairs={{0,2},{1,3},{2,0},{3,1},{4,6},{5,7},{6,4},{7,5},{8,10},{9,11},{10,... | collective-permute-start | bytes 393224 | tf_op jit(solution)/shard_map/ppermute | solution.py:362
  25.2 8.6 %collective-permute-start.14 = (bf16[128,512]{1,0:T(8,128)(2,1)S(1)}, bf16[128,512]{1,0:T(8,128)(2,1)S(1)}, u32[]{:S(2)}, u32[]{:S(2)}) collective-permute-start(bf16[128,512]{1,0:T(8,128)(2,1)S(1)} %collective-permute-done.13), channel_id=1, source_target_pairs={{0,2},{1,3},{2,0},{3,1},{4,6},{5,7},{6,4},{7,5},{8,10},{9,11},{10,... | collective-permute-start | bytes 393224 | tf_op jit(solution)/shard_map/ppermute | solution.py:362
  25.4 6.5 %collective-permute-start.9 = (bf16[64,512]{1,0:T(8,128)(2,1)S(1)}, bf16[64,512]{1,0:T(8,128)(2,1)S(1)}, u32[]{:S(2)}, u32[]{:S(2)}) collective-permute-start(bf16[64,512]{1,0:T(8,128)(2,1)S(1)} %get-tuple-element.28), channel_id=1, source_target_pairs={{0,8},{4,12},{8,0},{12,4},{16,24},{20,28},{24,16},{28,20},{1,9},{5... | collective-permute-start | bytes 196616 | tf_op jit(solution)/shard_map/ppermute | solution.py:367
  29.6 8.8 %collective-permute-start.7 = (bf16[128,512]{1,0:T(8,128)(2,1)S(1)}, bf16[128,512]{1,0:T(8,128)(2,1)S(1)}, u32[]{:S(2)}, u32[]{:S(2)}) collective-permute-start(bf16[128,512]{1,0:T(8,128)(2,1)S(1)} %pad_maximum_fusion.4), channel_id=1, source_target_pairs={{0,8},{4,12},{8,0},{12,4},{16,24},{20,28},{24,16},{28,20},{1,9},{5... | collective-permute-start | bytes 393224 | tf_op jit(solution)/shard_map/ppermute | solution.py:367
  31.9 8.5 %collective-permute-start.10 = (bf16[192,512]{1,0:T(8,128)(2,1)S(1)}, bf16[192,512]{1,0:T(8,128)(2,1)S(1)}, u32[]{:S(2)}, u32[]{:S(2)}) collective-permute-start(bf16[192,512]{1,0:T(8,128)(2,1)S(1)} %pad_maximum_fusion.3), channel_id=1, source_target_pairs={{0,4},{4,0},{8,12},{12,8},{16,20},{20,16},{24,28},{28,24},{1,5},{5... | collective-permute-start | bytes 589832 | tf_op jit(solution)/shard_map/ppermute | solution.py:367
  33.9 8.5 %collective-permute-start.15 = (bf16[4,128,512]{2,1,0:T(8,128)(2,1)S(1)}, bf16[4,128,512]{2,1,0:T(8,128)(2,1)S(1)}, u32[]{:S(2)}, u32[]{:S(2)}) collective-permute-start(bf16[4,128,512]{2,1,0:T(8,128)(2,1)S(1)} %pad_maximum_fusion.refs_0_), channel_id=1, source_target_pairs={{0,1},{1,0},{2,3},{3,2},{4,5},{5,4},{6,7},{7,6},{8,9},{9,8},{10,11... | collective-permute-start | bytes 1572872 | tf_op jit(solution)/shard_map/ppermute | solution.py:362
  38.5 9.6 %collective-permute-start.8 = (bf16[256,512]{1,0:T(8,128)(2,1)S(1)}, bf16[256,512]{1,0:T(8,128)(2,1)S(1)}, u32[]{:S(2)}, u32[]{:S(2)}) collective-permute-start(bf16[256,512]{1,0:T(8,128)(2,1)S(1)} %pad_maximum_fusion.1.refs_0_), channel_id=1, source_target_pairs={{0,4},{4,0},{8,12},{12,8},{16,20},{20,16},{24,28},{28,24},{1,5},{5... | collective-permute-start | bytes 786440 | tf_op jit(solution)/shard_map/ppermute | solution.py:367
  40.4 7.7 %collective-permute-start.11 = (bf16[256,512]{1,0:T(8,128)(2,1)S(1)}, bf16[256,512]{1,0:T(8,128)(2,1)S(1)}, u32[]{:S(2)}, u32[]{:S(2)}) collective-permute-start(bf16[256,512]{1,0:T(8,128)(2,1)S(1)} %pad_maximum_fusion.2.refs_0_), channel_id=1, source_target_pairs={{0,16},{4,20},{8,24},{12,28},{16,0},{20,4},{24,8},{28,12},{1,17},{... | collective-permute-start | bytes 786440 | tf_op jit(solution)/shard_map/ppermute | solution.py:367
  41.8 5.9 %collective-permute-start.16 = (bf16[64,512]{1,0:T(8,128)(2,1)S(1)}, bf16[64,512]{1,0:T(8,128)(2,1)S(1)}, u32[]{:S(2)}, u32[]{:S(2)}) collective-permute-start(bf16[64,512]{1,0:T(8,128)(2,1)S(1)} %add_convert_fusion.refs_6_), channel_id=1, source_target_pairs={{0,8},{4,12},{8,0},{12,4},{16,24},{20,28},{24,16},{28,20},{1,9},{5... | collective-permute-start | bytes 196616 | tf_op jit(solution)/shard_map/ppermute | solution.py:367
